TPU v7x, 256 devices: a whole 4x4x8 slice. The times are simulated.
256 devices in a mesh: section: 4 (over y_hi, core), tok: 16 (over z, y_lo), lat: 4 (over x).
Axes of the slice: x: 4, y: 4 (y_hi: 2, y_lo: 2; y = y_hi * 2 + y_lo), z: 8, core: 2. Of those that a mesh axis runs over, the one named last changes fastest.
Arguments:
- resid: bfloat16 [4, 2048, 4608], P('section', 'tok', 'lat'), may hold values from -6 to 6
- block_lists: int32 [4, 64, 32], P('section'), may hold values from 0 to 255, all different within a row; in each aligned block of 64 rows (0 to 63, 64 to 127, ..., all dimensions but the last counted through in order) at most 20 rows name the same one
- threshold_level: int32 [4, 32768], P('section', 'tok'), may hold values from 0 to 8
- w_enc: bfloat16 [4, 4608, 32768], P('section', 'lat', 'tok'), may hold values from -0.09375 to 0.09375
- w_dec: bfloat16 [4, 32768, 4608], P('section', 'tok', 'lat'), may hold values from -0.09375 to 0.09375
Outputs:
- reconstruction: bfloat16 [2048, 4608], P(('section', 'tok'), 'lat')
Inputs may be any that keep to these rules, and one draw needn't show every extreme that they name: `block_lists`: each row lists 32 different blocks. Within one source layer no block is named by more than 20 tiles, and some block is named by exactly 20 tiles.
All inputs are finite; a program needn't handle non-finite values.
Results may differ from a plain program's by a relative error of at most 0.0049.
Values may be sent and summed in bfloat16 or wider, within the bound.
No kernel may reach another device: no remote copies, remote signals or barrier semaphores. Data moves between devices by JAX's collectives and lax.ppermute only.
A program may use at most 128 MiB of HBM per device.

v0:
```python
import functools

import jax
import jax.numpy as jnp
from jax import lax
from jax.experimental import pallas as pl
from jax.experimental.pallas import tpu as pltpu
from jax.sharding import Mesh, PartitionSpec as P

BLOCK = 128
BPO = 16
TILE = 32
TILES = 64
WIDTH = 1152
SLOTS = 320
GROUP = 8
HALF_GROUP = 4
W_SPLIT = 4
FAST = 208
SCALE = 16.0
F32 = jnp.float32
BF16 = jnp.bfloat16
ENCODE_LIMIT = 20 << 20
DECODE_LIMIT = 24 << 20


def shift(axis, step, size):
    pairs = [(i, (i + step) % size) for i in range(size)]
    return lambda value: lax.ppermute(value, axis, pairs)


def gather_tokens(rows):
    up, down, swap = shift("z", 1, 8), shift("z", -1, 8), shift("yl", 1, 2)
    own, other = {0: rows}, {}
    own[-1], own[1], other[0] = up(own[0]), down(own[0]), swap(own[0])
    own[-2], own[2], other[-1] = up(own[-1]), down(own[1]), swap(own[-1])
    own[-3], own[3], other[1] = up(own[-2]), down(own[2]), swap(own[1])
    own[4], other[2], other[-2] = up(own[-3]), down(other[1]), swap(own[-2])
    other[-3], other[3], other[4] = up(other[-2]), down(other[2]), swap(own[4])
    order = (0, 1, 2, 3, 4, -3, -2, -1)
    return [own[d] for d in order] + [other[d] for d in order]


def make_tables(lists, places):
    y = places["yh"] * 2 + places["yl"]
    tok = places["z"] * 2 + places["yl"]
    block = jnp.arange(BPO, dtype=jnp.int32)
    named = jnp.any(lists[None] == (tok * BPO + block)[:, None, None], axis=2)
    tile = jnp.arange(TILES, dtype=jnp.int32)
    near = ((tile >> 4) & 1) ^ places["core"] ^ 1
    key = near * TILES + tile
    before = jnp.dot(named.astype(F32), (key[:, None] < key[None, :]).astype(F32))
    counts = jnp.sum(named.astype(jnp.int32), axis=1)
    far = jnp.sum(jnp.where(near[None, :] == 0, named.astype(jnp.int32), 0), axis=1)
    ends = jnp.sum(jnp.where(block[None, :] <= block[:, None], counts[None, :], 0), axis=1)
    starts = ends - counts
    rank = jnp.where(named, before.astype(jnp.int32) + starts[:, None], -1)
    source = ((((tile >> 2) & 1) ^ places["yl"]) * 8 + (((tile >> 3) - places["z"]) & 7)) * 4 + (tile & 3)
    target = ((((tile >> 5) * 2 + (tile & 1)) - y) & 3) * 8 + ((((tile >> 1) & 7) - places["z"]) & 7)
    code = source + 128 * target
    slot = jnp.arange(SLOTS + 2 * GROUP, dtype=jnp.int32)
    hit = rank.reshape(1, -1) == slot[:, None]
    found = jnp.sum(jnp.where(hit, jnp.tile(code, BPO)[None, :], 0), axis=1)
    table = found + 16384 * jnp.where(slot < FAST, turned(slot, 0, FAST, places), turned(slot, FAST, SLOTS, places))
    return table, jnp.concatenate([starts, starts + far, ends])


def turned(slot, low, high, places):
    part = (high - low) // 4
    quarter = (slot - low) // part
    return low + ((quarter - places["x"]) & 3) * part + slot - low - quarter * part


def encode_kernel(low, high, table, offsets, *refs):
    shards, (w_hbm, out_ref, rows, w_buf, lhs, sem, w_sem) = refs[:16], refs[16:]
    wide = W_SPLIT * BLOCK
    copies = [pltpu.make_async_copy(s, rows.at[pl.ds(4 * i, 4)], sem.at[i]) for i, s in enumerate(shards)]
    loads = [
        pltpu.make_async_copy(w_hbm.at[:, pl.ds(i * wide, wide)], w_buf.at[i], w_sem.at[i])
        for i in range(BPO // W_SPLIT)
    ]
    for c in copies + loads:
        c.start()
    for c in copies + loads:
        c.wait()

    def block(index, carry):
        first = jnp.maximum(offsets[index], low)
        last = jnp.minimum(offsets[2 * BPO + index], high)
        outer = index // W_SPLIT
        column = pl.ds(pl.multiple_of((index - outer * W_SPLIT) * BLOCK, BLOCK), BLOCK)

        def group(g, carry):
            base = first + g * GROUP
            codes = [table[base + u] for u in range(GROUP)]
            for u in range(GROUP):
                lhs[pl.ds(u * TILE, TILE), :] = rows[codes[u] & 127]
            part = jnp.dot(lhs[...], w_buf[outer, :, column], preferred_element_type=F32)
            for u in range(GROUP):
                row = jnp.where(base + u < last, (codes[u] >> 14) - low, high - low)
                out_ref[row] = part[u * TILE : (u + 1) * TILE]
            return carry

        return lax.fori_loop(0, (last - first + GROUP - 1) // GROUP, group, carry)

    lax.fori_loop(0, BPO, block, 0)


def encode(low, high, table, offsets, shards, w_enc):
    return pl.pallas_call(
        functools.partial(encode_kernel, low, high),
        out_shape=jax.ShapeDtypeStruct((high - low + 1, TILE, BLOCK), F32),
        grid_spec=pltpu.PrefetchScalarGridSpec(
            num_scalar_prefetch=2,
            grid=(),
            in_specs=[pl.BlockSpec(memory_space=pl.ANY)] * 17,
            out_specs=pl.BlockSpec(memory_space=pltpu.VMEM),
            scratch_shapes=[
                pltpu.VMEM((TILES, TILE, WIDTH), BF16),
                pltpu.VMEM((BPO // W_SPLIT, WIDTH, W_SPLIT * BLOCK), BF16),
                pltpu.VMEM((GROUP * TILE, WIDTH), BF16),
                pltpu.SemaphoreType.DMA((16,)),
                pltpu.SemaphoreType.DMA((BPO // W_SPLIT,)),
            ],
        ),
        compiler_params=pltpu.CompilerParams(vmem_limit_bytes=ENCODE_LIMIT),
        name="encode",
    )(table, offsets, *[s.reshape(4, TILE, WIDTH) for s in shards], w_enc)


def decode_kernel(near, table, offsets, *refs):
    pieces, (w_hbm, out_ref, acts, w_buf, lhs, total, sem, w_sem) = refs[:8], refs[8:]
    half = TILES // 2
    copies, at = [], 0
    for i, p in enumerate(pieces):
        copies.append(pltpu.make_async_copy(p, acts.at[pl.ds(at, p.shape[0])], sem.at[i]))
        at += p.shape[0]
    lines = BPO * BLOCK // W_SPLIT
    loads = [
        pltpu.make_async_copy(w_hbm.at[pl.ds(i * lines, lines)], w_buf.at[pl.ds(i * lines, lines)], w_sem.at[i])
        for i in range(W_SPLIT)
    ]
    for c in copies + loads:
        c.start()
    total[...] = jnp.zeros_like(total)
    for c in copies + loads:
        c.wait()

    def block(index, carry):
        first, last = offsets[near * BPO + index], offsets[(near + 1) * BPO + index]
        line = pl.ds(pl.multiple_of(index * BLOCK, BLOCK), BLOCK)

        def group(g, carry):
            base = first + g * HALF_GROUP
            codes = [table[base + u] for u in range(HALF_GROUP)]
            for u in range(HALF_GROUP):
                row = jnp.where(base + u < last, codes[u] >> 14, 0)
                lhs[pl.ds(u * TILE, TILE), :] = acts[row]
            part = jnp.dot(lhs[...], w_buf[line, :], preferred_element_type=F32)
            for u in range(HALF_GROUP):
                tile = jnp.where(base + u < last, (codes[u] >> 7) & 127, half)
                total[tile] += part[u * TILE : (u + 1) * TILE]
            return carry

        return lax.fori_loop(0, (last - first + HALF_GROUP - 1) // HALF_GROUP, group, carry)

    lax.fori_loop(0, BPO, block, 0)
    out_ref[...] = total[0:half].astype(out_ref.dtype)


def decode(near, table, offsets, pieces, w_dec):
    return pl.pallas_call(
        functools.partial(decode_kernel, near),
        out_shape=jax.ShapeDtypeStruct((TILES // 2, TILE, WIDTH), F32 if near else BF16),
        grid_spec=pltpu.PrefetchScalarGridSpec(
            num_scalar_prefetch=2,
            grid=(),
            in_specs=[pl.BlockSpec(memory_space=pl.ANY)] * 9,
            out_specs=pl.BlockSpec(memory_space=pltpu.VMEM),
            scratch_shapes=[
                pltpu.VMEM((SLOTS, TILE, BLOCK), BF16),
                pltpu.VMEM((BPO * BLOCK, WIDTH), BF16),
                pltpu.VMEM((HALF_GROUP * TILE, BLOCK), BF16),
                pltpu.VMEM((TILES // 2 + 1, TILE, WIDTH), F32),
                pltpu.SemaphoreType.DMA((8,)),
                pltpu.SemaphoreType.DMA((W_SPLIT,)),
            ],
        ),
        compiler_params=pltpu.CompilerParams(vmem_limit_bytes=DECODE_LIMIT),
        name="decode_near" if near else "decode_far",
    )(table, offsets, *pieces, w_dec)


def activate(low, high, table, offsets, thresholds, w_enc, places, *shards):
    right, left, across = shift("x", 1, 4), shift("x", -1, 4), shift("x", 2, 4)
    part = (high - low) // 4
    pre = encode(low, high, table, offsets, shards, w_enc)
    quarters = [pre[r * part : (r + 1) * part] for r in range(4)]
    sent = [(q * SCALE).astype(jnp.float16) for q in quarters[1:]]
    got = [right(sent[0]), across(sent[1]), left(sent[2])]
    mine = low + places["x"] * part + jnp.arange(part, dtype=jnp.int32)
    block = jnp.sum((mine[:, None] >= offsets[None, 2 * BPO :]).astype(jnp.int32), axis=1)
    pick = (block[:, None] == jnp.arange(BPO, dtype=jnp.int32)[None, :]).astype(F32)
    limits = jnp.dot(pick, thresholds.astype(F32) * 0.125, precision=lax.Precision.HIGHEST)
    summed = quarters[0] + (got[0].astype(F32) + got[1].astype(F32) + got[2].astype(F32)) * (1.0 / SCALE)
    acts = jnp.maximum(summed - limits[:, None, :], 0.0).astype(BF16)
    return acts, left(acts), across(acts), right(acts)


def no_more(table, offsets, thresholds, w_enc, places, *shards):
    return (jnp.zeros(((SLOTS - FAST) // 4, TILE, BLOCK), BF16),) * 4


def reduce_tokens(mine, other):
    y = ("yh", "yl")
    mine = mine.reshape(4, 8, TILE, WIDTH)
    other = other.reshape(4, 8, TILE, WIDTH)
    sent = [(mine[r] + other[r].astype(F32)).astype(BF16) for r in (2, 1, 3)]
    got = [shift(y, r, 4)(s) for r, s in zip((2, 1, 3), sent)]
    column = mine[0] + other[0].astype(F32) + got[0].astype(F32) + got[1].astype(F32) + got[2].astype(F32)
    ways = (4, 3, 5, 2, 6, 1, 7)
    sent = [column[d].astype(BF16) for d in ways]
    got = [shift("z", d, 8)(s) for d, s in zip(ways, sent)]
    result = column[0]
    for g in got:
        result = result + g.astype(F32)
    return result.astype(BF16)


def shards(resid, block_lists, threshold_level, w_enc, w_dec):
    places = {name: lax.axis_index(name) for name in ("yh", "core", "z", "yl", "x")}
    table, offsets = make_tables(block_lists[0], places)
    gathered = gather_tokens(resid[0])
    operands = (table, offsets, threshold_level[0].reshape(BPO, BLOCK), w_enc[0], places, *gathered)
    pieces = activate(0, FAST, *operands)
    more = lax.cond(offsets[3 * BPO - 1] > FAST, functools.partial(activate, FAST, SLOTS), no_more, *operands)
    pieces = pieces + tuple(more)
    other = shift("core", 1, 2)(decode(0, table, offsets, pieces, w_dec[0]))
    return reduce_tokens(decode(1, table, offsets, pieces, w_dec[0]), other)


def solution(mesh):
    section, tok, lat = ("yh", "core"), ("z", "yl"), "x"
    fine = Mesh(mesh.devices.reshape(2, 2, 8, 2, 4), section + tok + (lat,))
    return jax.shard_map(
        shards,
        mesh=fine,
        in_specs=(
            P(section, tok, lat),
            P(section, None, None),
            P(section, tok),
            P(section, lat, tok),
            P(section, tok, lat),
        ),
        out_specs=P(section + tok, lat),
        check_vma=False,
    )
```

profile of v0, /device:TPU:8, one launch (start us, length us, event | category | flops | bytes accessed | tf_op | source)
XLA Modules:
  0.0 181.9 jit_solution(8483162105216605799)
XLA Ops:
  0.0 1.9 %collective-permute-start.9 = (bf16[128,1152]{1,0:T(8,128)(2,1)}, bf16[128,1152]{1,0:T(8,128)(2,1)S(1)}, u32[]{:S(2)}, u32[]{:S(2)}) collective-permute-start(bf16[128,1152]{1,0:T(8,128)(2,1)} %bitcast.75), channel_id=1, source_target_pairs={{0,8},{8,16},{16,24},{24,32},{32,40},{40,48},{48,56},{56,0},{1,9},... | collective-permute-start | bytes 884744 | tf_op jit(solution)/shard_map/ppermute | solution.py:29
  2.4 3.9 %collective-permute-start.6 = (bf16[128,1152]{1,0:T(8,128)(2,1)}, bf16[128,1152]{1,0:T(8,128)(2,1)S(1)}, u32[]{:S(2)}, u32[]{:S(2)}) collective-permute-start(bf16[128,1152]{1,0:T(8,128)(2,1)} %bitcast.77), channel_id=1, source_target_pairs={{0,56},{8,0},{16,8},{24,16},{32,24},{40,32},{48,40},{56,48},{1,57}... | collective-permute-start | bytes 884744 | tf_op jit(solution)/shard_map/ppermute | solution.py:29
  7.2 5.9 %collective-permute-done.9 = bf16[128,1152]{1,0:T(8,128)(2,1)S(1)} collective-permute-done((bf16[128,1152]{1,0:T(8,128)(2,1)}, bf16[128,1152]{1,0:T(8,128)(2,1)S(1)}, u32[]{:S(2)}, u32[]{:S(2)}) %collective-permute-start.9) | collective-permute-done | bytes 294944 | tf_op jit(solution)/shard_map/ppermute | solution.py:29
  14.2 8.3 %collective-permute-done.10 = bf16[128,1152]{1,0:T(8,128)(2,1)S(1)} collective-permute-done((bf16[128,1152]{1,0:T(8,128)(2,1)S(1)}, bf16[128,1152]{1,0:T(8,128)(2,1)S(1)}, u32[]{:S(2)}, u32[]{:S(2)}) %collective-permute-start.10) | collective-permute-done | bytes 294944 | tf_op jit(solution)/shard_map/ppermute | solution.py:29
  22.5 3.3 %collective-permute-start.7 = (bf16[128,1152]{1,0:T(8,128)(2,1)S(1)}, bf16[128,1152]{1,0:T(8,128)(2,1)S(1)}, u32[]{:S(2)}, u32[]{:S(2)}) collective-permute-start(bf16[128,1152]{1,0:T(8,128)(2,1)S(1)} %collective-permute-done.6), channel_id=1, source_target_pairs={{0,56},{8,0},{16,8},{24,16},{32,24},{40,32},{48,40},{56,48},{1,57}... | collective-permute-start | bytes 884744 | tf_op jit(solution)/shard_map/ppermute | solution.py:29
  26.4 4.6 %collective-permute-done.11 = bf16[128,1152]{1,0:T(8,128)(2,1)S(1)} collective-permute-done((bf16[128,1152]{1,0:T(8,128)(2,1)S(1)}, bf16[128,1152]{1,0:T(8,128)(2,1)S(1)}, u32[]{:S(2)}, u32[]{:S(2)}) %collective-permute-start.11) | collective-permute-done | bytes 294944 | tf_op jit(solution)/shard_map/ppermute | solution.py:29
  33.4 3.6 %collective-permute-start.8 = (bf16[128,1152]{1,0:T(8,128)(2,1)S(1)}, bf16[128,1152]{1,0:T(8,128)(2,1)S(1)}, u32[]{:S(2)}, u32[]{:S(2)}) collective-permute-start(bf16[128,1152]{1,0:T(8,128)(2,1)S(1)} %collective-permute-done.7), channel_id=1, source_target_pairs={{0,56},{8,0},{16,8},{24,16},{32,24},{40,32},{48,40},{56,48},{1,57}... | collective-permute-start | bytes 884744 | tf_op jit(solution)/shard_map/ppermute | solution.py:29
  37.0 2.6 %collective-permute-done.15 = bf16[128,1152]{1,0:T(8,128)(2,1)S(1)} collective-permute-done((bf16[128,1152]{1,0:T(8,128)(2,1)S(1)}, bf16[128,1152]{1,0:T(8,128)(2,1)S(1)}, u32[]{:S(2)}, u32[]{:S(2)}) %collective-permute-start.15) | collective-permute-done | bytes 294944 | tf_op jit(solution)/shard_map/ppermute | solution.py:29
  39.6 3.7 %collective-permute-start.16 = (bf16[128,1152]{1,0:T(8,128)(2,1)S(1)}, bf16[128,1152]{1,0:T(8,128)(2,1)S(1)}, u32[]{:S(2)}, u32[]{:S(2)}) collective-permute-start(bf16[128,1152]{1,0:T(8,128)(2,1)S(1)} %collective-permute-done.15), channel_id=1, source_target_pairs={{0,56},{8,0},{16,8},{24,16},{32,24},{40,32},{48,40},{56,48},{1,57}... | collective-permute-start | bytes 884744 | tf_op jit(solution)/shard_map/ppermute | solution.py:29
  43.4 2.5 %collective-permute-done.8 = bf16[128,1152]{1,0:T(8,128)(2,1)S(1)} collective-permute-done((bf16[128,1152]{1,0:T(8,128)(2,1)S(1)}, bf16[128,1152]{1,0:T(8,128)(2,1)S(1)}, u32[]{:S(2)}, u32[]{:S(2)}) %collective-permute-start.8) | collective-permute-done | bytes 294944 | tf_op jit(solution)/shard_map/ppermute | solution.py:29
  45.9 3.4 %collective-permute-done.16 = bf16[128,1152]{1,0:T(8,128)(2,1)S(1)} collective-permute-done((bf16[128,1152]{1,0:T(8,128)(2,1)S(1)}, bf16[128,1152]{1,0:T(8,128)(2,1)S(1)}, u32[]{:S(2)}, u32[]{:S(2)}) %collective-permute-start.16) | collective-permute-done | bytes 294944 | tf_op jit(solution)/shard_map/ppermute | solution.py:29
  50.1 11.7 %encode.3 = f32[209,32,128]{2,1,0:T(8,128)S(1)} custom-call(s32[336]{0:T(512)S(1)} %multiply_add_fusion.table, s32[48]{0:T(128)S(1)} %pad_add_fusion.offsets, bf16[4,32,1152]{2,1,0:T(8,128)(2,1)} %bitcast.78, bf16[4,32,1152]{2,1,0:T(8,128)(2,1)} %bitcast.84, bf16[4,32,1152]{2,1,0:T(8,128)(2,1)} %bitcast.92, bf16[4,32,1152]{2,1,0:T(8,128)(2,1)S(1)} %bitcast.102, ...), custom_call_target="tpu_custom_call" | custom-call | tf_op jit(solution)/shard_map/encode/pallas_call | solution.py:110
  64.6 1.8 collective-permute-start.23
  66.5 3.0 %conditional.1 = (bf16[28,32,128]{2,1,0:T(8,128)(2,1)}, bf16[28,32,128]{2,1,0:T(8,128)(2,1)}, bf16[28,32,128]{2,1,0:T(8,128)(2,1)}, bf16[28,32,128]{2,1,0:T(8,128)(2,1)}) conditional(s32[]{:T(128)} %bitcast.36, () %tuple.13, (bf16[1,128,1152]{2,1,0:T(8,128)(2,1)S(1)}, bf16[128,1152]{1,0:T(8,128)(2,1)S(1)}, bf16[128,1152]{1,0:T(8,128)(2,1)S(1)}, ...), branch_computations={%region_6.7_spmd, %region_7.9_spmd} | conditional | flops 2529026 | bytes 16388936 | solution.py:236
  69.5 1.8 collective-permute-start.22
  71.6 4.6 %collective-permute-done.21 = f16[52,32,128]{2,1,0:T(8,128)(2,1)} collective-permute-done((f16[52,32,128]{2,1,0:T(8,128)(2,1)}, f16[52,32,128]{2,1,0:T(8,128)(2,1)}, u32[]{:S(2)}, u32[]{:S(2)}) %collective-permute-start.21) | collective-permute-done | bytes 426016 | tf_op jit(solution)/shard_map/ppermute | solution.py:29
  77.4 5.4 %collective-permute-done.22 = f16[52,32,128]{2,1,0:T(8,128)(2,1)S(1)} collective-permute-done((f16[52,32,128]{2,1,0:T(8,128)(2,1)}, f16[52,32,128]{2,1,0:T(8,128)(2,1)S(1)}, u32[]{:S(2)}, u32[]{:S(2)}) %collective-permute-start.22) | collective-permute-done | bytes 426016 | tf_op jit(solution)/shard_map/ppermute | solution.py:29
  85.2 2.6 %collective-permute-start.25 = (bf16[52,32,128]{2,1,0:T(8,128)(2,1)S(1)}, bf16[52,32,128]{2,1,0:T(8,128)(2,1)S(1)}, u32[]{:S(2)}, u32[]{:S(2)}) collective-permute-start(bf16[52,32,128]{2,1,0:T(8,128)(2,1)S(1)} %fusion.25.refs_0_), channel_id=1, source_target_pairs={{0,2},{1,3},{2,0},{3,1},{4,6},{5,7},{6,4},{7,5},{8,10},{9,11},{10,... | collective-permute-start | bytes 1277960 | tf_op jit(solution)/shard_map/ppermute | solution.py:29
  88.0 14.2 %collective-permute-done.26.refs_3_ = bf16[52,32,128]{2,1,0:T(8,128)(2,1)S(1)} collective-permute-done((bf16[52,32,128]{2,1,0:T(8,128)(2,1)S(1)}, bf16[52,32,128]{2,1,0:T(8,128)(2,1)S(1)}, u32[]{:S(2)}, u32[]{:S(2)}) %collective-permute-start.26) | collective-permute-done | bytes 426016 | tf_op jit(solution)/shard_map/ppermute | solution.py:29
  102.8 2.3 %copy-done = bf16[1,2048,1152]{2,1,0:T(8,128)(2,1)S(1)} copy-done((bf16[1,2048,1152]{2,1,0:T(8,128)(2,1)S(1)}, bf16[1,2048,1152]{2,1,0:T(8,128)(2,1)}, u32[]{:S(2)}) %copy-start) | copy-done | bytes 4718616
  105.1 8.8 %decode_far.1 = bf16[32,32,1152]{2,1,0:T(8,128)(2,1)S(1)} custom-call(s32[336]{0:T(512)S(1)} %multiply_add_fusion.table, s32[48]{0:T(128)S(1)} %pad_add_fusion.offsets, bf16[52,32,128]{2,1,0:T(8,128)(2,1)S(1)} %fusion.25.refs_0_, bf16[52,32,128]{2,1,0:T(8,128)(2,1)S(1)} %collective-permute-done.24.refs_1_, ...), custom_call_target="tpu_custom_call" | custom-call | tf_op jit(solution)/shard_map/decode_far/pallas_call | solution.py:172
  114.2 9.1 %decode_near.1 = f32[32,32,1152]{2,1,0:T(8,128)S(1)} custom-call(s32[336]{0:T(512)S(1)} %multiply_add_fusion.table, s32[48]{0:T(128)S(1)} %pad_add_fusion.offsets, bf16[52,32,128]{2,1,0:T(8,128)(2,1)S(1)} %fusion.25.refs_0_, bf16[52,32,128]{2,1,0:T(8,128)(2,1)S(1)} %collective-permute-done.24.refs_1_, ...), custom_call_target="tpu_custom_call" | custom-call | tf_op jit(solution)/shard_map/decode_near/pallas_call | solution.py:172
  123.8 3.2 %collective-permute-start.28 = (bf16[8,32,1152]{2,1,0:T(8,128)(2,1)S(1)}, bf16[8,32,1152]{2,1,0:T(8,128)(2,1)S(1)}, u32[]{:S(2)}, u32[]{:S(2)}) collective-permute-start(bf16[8,32,1152]{2,1,0:T(8,128)(2,1)S(1)} %get-tuple-element.88), channel_id=1, source_target_pairs={{0,128},{4,132},{128,0},{132,4},{1,129},{5,133},{129,1},{133,5},{2... | collective-permute-start | bytes 1769480 | tf_op jit(solution)/shard_map/ppermute | solution.py:29
  129.0 12.5 %collective-permute-done.28 = bf16[8,32,1152]{2,1,0:T(8,128)(2,1)S(1)} collective-permute-done((bf16[8,32,1152]{2,1,0:T(8,128)(2,1)S(1)}, bf16[8,32,1152]{2,1,0:T(8,128)(2,1)S(1)}, u32[]{:S(2)}, u32[]{:S(2)}) %collective-permute-start.28) | collective-permute-done | bytes 589856 | tf_op jit(solution)/shard_map/ppermute | solution.py:29
  141.5 12.1 %collective-permute-done.30 = bf16[8,32,1152]{2,1,0:T(8,128)(2,1)S(1)} collective-permute-done((bf16[8,32,1152]{2,1,0:T(8,128)(2,1)S(1)}, bf16[8,32,1152]{2,1,0:T(8,128)(2,1)S(1)}, u32[]{:S(2)}, u32[]{:S(2)}) %collective-permute-start.30) | collective-permute-done | bytes 589856 | tf_op jit(solution)/shard_map/ppermute | solution.py:29
  153.6 1.6 collective-permute-done.29
  155.6 9.5 %collective-permute-start.31 = (bf16[32,1152]{1,0:T(8,128)(2,1)S(1)}, bf16[32,1152]{1,0:T(8,128)(2,1)S(1)}, u32[]{:S(2)}, u32[]{:S(2)}) collective-permute-start(bf16[32,1152]{1,0:T(8,128)(2,1)S(1)} %get-tuple-element.94), channel_id=1, source_target_pairs={{0,32},{8,40},{16,48},{24,56},{32,0},{40,8},{48,16},{56,24},{1,33}... | collective-permute-start | bytes 221192 | tf_op jit(solution)/shard_map/ppermute | solution.py:29
  165.1 2.0 %collective-permute-start.36 = (bf16[32,1152]{1,0:T(8,128)(2,1)S(1)}, bf16[32,1152]{1,0:T(8,128)(2,1)S(1)}, u32[]{:S(2)}, u32[]{:S(2)}) collective-permute-start(bf16[32,1152]{1,0:T(8,128)(2,1)S(1)} %get-tuple-element.96), channel_id=1, source_target_pairs={{0,8},{8,16},{16,24},{24,32},{32,40},{40,48},{48,56},{56,0},{1,9},... | collective-permute-start | bytes 221192 | tf_op jit(solution)/shard_map/ppermute | solution.py:29
  167.1 2.9 %collective-permute-start.34 = (bf16[32,1152]{1,0:T(8,128)(2,1)S(1)}, bf16[32,1152]{1,0:T(8,128)(2,1)S(1)}, u32[]{:S(2)}, u32[]{:S(2)}) collective-permute-start(bf16[32,1152]{1,0:T(8,128)(2,1)S(1)} %get-tuple-element.98), channel_id=1, source_target_pairs={{0,16},{8,24},{16,32},{24,40},{32,48},{40,56},{48,0},{56,8},{1,17}... | collective-permute-start | bytes 221192 | tf_op jit(solution)/shard_map/ppermute | solution.py:29
  170.0 2.2 %collective-permute-start.33 = (bf16[32,1152]{1,0:T(8,128)(2,1)S(1)}, bf16[32,1152]{1,0:T(8,128)(2,1)S(1)}, u32[]{:S(2)}, u32[]{:S(2)}) collective-permute-start(bf16[32,1152]{1,0:T(8,128)(2,1)S(1)} %get-tuple-element.99), channel_id=1, source_target_pairs={{0,40},{8,48},{16,56},{24,0},{32,8},{40,16},{48,24},{56,32},{1,41}... | collective-permute-start | bytes 221192 | tf_op jit(solution)/shard_map/ppermute | solution.py:29
  173.9 4.0 %collective-permute-done.33 = bf16[32,1152]{1,0:T(8,128)(2,1)S(1)} collective-permute-done((bf16[32,1152]{1,0:T(8,128)(2,1)S(1)}, bf16[32,1152]{1,0:T(8,128)(2,1)S(1)}, u32[]{:S(2)}, u32[]{:S(2)}) %collective-permute-start.33) | collective-permute-done | bytes 73760 | tf_op jit(solution)/shard_map/ppermute | solution.py:29
  177.9 3.3 %collective-permute-done.32 = bf16[32,1152]{1,0:T(8,128)(2,1)S(1)} collective-permute-done((bf16[32,1152]{1,0:T(8,128)(2,1)S(1)}, bf16[32,1152]{1,0:T(8,128)(2,1)S(1)}, u32[]{:S(2)}, u32[]{:S(2)}) %collective-permute-start.32) | collective-permute-done | bytes 73760 | tf_op jit(solution)/shard_map/ppermute | solution.py:29
  (113 shorter events, 21.5 us)
Async XLA Ops:
  0.0 13.1 %collective-permute-start.9 = (bf16[128,1152]{1,0:T(8,128)(2,1)}, bf16[128,1152]{1,0:T(8,128)(2,1)S(1)}, u32[]{:S(2)}, u32[]{:S(2)}) collective-permute-start(bf16[128,1152]{1,0:T(8,128)(2,1)} %bitcast.75), channel_id=1, source_target_pairs={{0,8},{8,16},{16,24},{24,32},{32,40},{40,48},{48,56},{56,0},{1,9},... | collective-permute-start | bytes 884744 | tf_op jit(solution)/shard_map/ppermute | solution.py:29
  1.9 30.9 %collective-permute-start.13 = (bf16[128,1152]{1,0:T(8,128)(2,1)}, bf16[128,1152]{1,0:T(8,128)(2,1)S(1)}, u32[]{:S(2)}, u32[]{:S(2)}) collective-permute-start(bf16[128,1152]{1,0:T(8,128)(2,1)} %bitcast.76), channel_id=1, source_target_pairs={{0,4},{4,0},{1,5},{5,1},{2,6},{6,2},{3,7},{7,3},{8,12},{12,8},{9,1... | collective-permute-start | bytes 884744 | tf_op jit(solution)/shard_map/ppermute | solution.py:29
  2.4 11.0 %collective-permute-start.6 = (bf16[128,1152]{1,0:T(8,128)(2,1)}, bf16[128,1152]{1,0:T(8,128)(2,1)S(1)}, u32[]{:S(2)}, u32[]{:S(2)}) collective-permute-start(bf16[128,1152]{1,0:T(8,128)(2,1)} %bitcast.77), channel_id=1, source_target_pairs={{0,56},{8,0},{16,8},{24,16},{32,24},{40,32},{48,40},{56,48},{1,57}... | collective-permute-start | bytes 884744 | tf_op jit(solution)/shard_map/ppermute | solution.py:29
  13.1 9.4 %collective-permute-start.10 = (bf16[128,1152]{1,0:T(8,128)(2,1)S(1)}, bf16[128,1152]{1,0:T(8,128)(2,1)S(1)}, u32[]{:S(2)}, u32[]{:S(2)}) collective-permute-start(bf16[128,1152]{1,0:T(8,128)(2,1)S(1)} %collective-permute-done.9), channel_id=1, source_target_pairs={{0,8},{8,16},{16,24},{24,32},{32,40},{40,48},{48,56},{56,0},{1,9},... | collective-permute-start | bytes 884744 | tf_op jit(solution)/shard_map/ppermute | solution.py:29
  13.3 12.9 %collective-permute-start.14 = (bf16[128,1152]{1,0:T(8,128)(2,1)S(1)}, bf16[128,1152]{1,0:T(8,128)(2,1)S(1)}, u32[]{:S(2)}, u32[]{:S(2)}) collective-permute-start(bf16[128,1152]{1,0:T(8,128)(2,1)S(1)} %collective-permute-done.6), channel_id=1, source_target_pairs={{0,4},{4,0},{1,5},{5,1},{2,6},{6,2},{3,7},{7,3},{8,12},{12,8},{9,1... | collective-permute-start | bytes 884744 | tf_op jit(solution)/shard_map/ppermute | solution.py:29
  22.5 8.5 %collective-permute-start.11 = (bf16[128,1152]{1,0:T(8,128)(2,1)S(1)}, bf16[128,1152]{1,0:T(8,128)(2,1)S(1)}, u32[]{:S(2)}, u32[]{:S(2)}) collective-permute-start(bf16[128,1152]{1,0:T(8,128)(2,1)S(1)} %collective-permute-done.10), channel_id=1, source_target_pairs={{0,8},{8,16},{16,24},{24,32},{32,40},{40,48},{48,56},{56,0},{1,9},... | collective-permute-start | bytes 884744 | tf_op jit(solution)/shard_map/ppermute | solution.py:29
  22.5 10.9 %collective-permute-start.7 = (bf16[128,1152]{1,0:T(8,128)(2,1)S(1)}, bf16[128,1152]{1,0:T(8,128)(2,1)S(1)}, u32[]{:S(2)}, u32[]{:S(2)}) collective-permute-start(bf16[128,1152]{1,0:T(8,128)(2,1)S(1)} %collective-permute-done.6), channel_id=1, source_target_pairs={{0,56},{8,0},{16,8},{24,16},{32,24},{40,32},{48,40},{56,48},{1,57}... | collective-permute-start | bytes 884744 | tf_op jit(solution)/shard_map/ppermute | solution.py:29
  25.8 11.2 %collective-permute-start.18 = (bf16[128,1152]{1,0:T(8,128)(2,1)S(1)}, bf16[128,1152]{1,0:T(8,128)(2,1)S(1)}, u32[]{:S(2)}, u32[]{:S(2)}) collective-permute-start(bf16[128,1152]{1,0:T(8,128)(2,1)S(1)} %collective-permute-done.10), channel_id=1, source_target_pairs={{0,4},{4,0},{1,5},{5,1},{2,6},{6,2},{3,7},{7,3},{8,12},{12,8},{9,1... | collective-permute-start | bytes 884744 | tf_op jit(solution)/shard_map/ppermute | solution.py:29
  26.3 13.3 %collective-permute-start.15 = (bf16[128,1152]{1,0:T(8,128)(2,1)S(1)}, bf16[128,1152]{1,0:T(8,128)(2,1)S(1)}, u32[]{:S(2)}, u32[]{:S(2)}) collective-permute-start(bf16[128,1152]{1,0:T(8,128)(2,1)S(1)} %collective-permute-done.14), channel_id=1, source_target_pairs={{0,56},{8,0},{16,8},{24,16},{32,24},{40,32},{48,40},{56,48},{1,57}... | collective-permute-start | bytes 884744 | tf_op jit(solution)/shard_map/ppermute | solution.py:29
  31.0 12.3 %collective-permute-start.12 = (bf16[128,1152]{1,0:T(8,128)(2,1)S(1)}, bf16[128,1152]{1,0:T(8,128)(2,1)S(1)}, u32[]{:S(2)}, u32[]{:S(2)}) collective-permute-start(bf16[128,1152]{1,0:T(8,128)(2,1)S(1)} %collective-permute-done.11), channel_id=1, source_target_pairs={{0,8},{8,16},{16,24},{24,32},{32,40},{40,48},{48,56},{56,0},{1,9},... | collective-permute-start | bytes 884744 | tf_op jit(solution)/shard_map/ppermute | solution.py:29
  32.8 10.6 %collective-permute-start.20 = (bf16[128,1152]{1,0:T(8,128)(2,1)S(1)}, bf16[128,1152]{1,0:T(8,128)(2,1)S(1)}, u32[]{:S(2)}, u32[]{:S(2)}) collective-permute-start(bf16[128,1152]{1,0:T(8,128)(2,1)S(1)} %collective-permute-done.9), channel_id=1, source_target_pairs={{0,4},{4,0},{1,5},{5,1},{2,6},{6,2},{3,7},{7,3},{8,12},{12,8},{9,1... | collective-permute-start | bytes 884744 | tf_op jit(solution)/shard_map/ppermute | solution.py:29
  33.4 12.5 %collective-permute-start.8 = (bf16[128,1152]{1,0:T(8,128)(2,1)S(1)}, bf16[128,1152]{1,0:T(8,128)(2,1)S(1)}, u32[]{:S(2)}, u32[]{:S(2)}) collective-permute-start(bf16[128,1152]{1,0:T(8,128)(2,1)S(1)} %collective-permute-done.7), channel_id=1, source_target_pairs={{0,56},{8,0},{16,8},{24,16},{32,24},{40,32},{48,40},{56,48},{1,57}... | collective-permute-start | bytes 884744 | tf_op jit(solution)/shard_map/ppermute | solution.py:29
  37.0 8.9 %collective-permute-start.19 = (bf16[128,1152]{1,0:T(8,128)(2,1)S(1)}, bf16[128,1152]{1,0:T(8,128)(2,1)S(1)}, u32[]{:S(2)}, u32[]{:S(2)}) collective-permute-start(bf16[128,1152]{1,0:T(8,128)(2,1)S(1)} %collective-permute-done.18), channel_id=1, source_target_pairs={{0,8},{8,16},{16,24},{24,32},{32,40},{40,48},{48,56},{56,0},{1,9},... | collective-permute-start | bytes 884744 | tf_op jit(solution)/shard_map/ppermute | solution.py:29
  39.6 9.7 %collective-permute-start.16 = (bf16[128,1152]{1,0:T(8,128)(2,1)S(1)}, bf16[128,1152]{1,0:T(8,128)(2,1)S(1)}, u32[]{:S(2)}, u32[]{:S(2)}) collective-permute-start(bf16[128,1152]{1,0:T(8,128)(2,1)S(1)} %collective-permute-done.15), channel_id=1, source_target_pairs={{0,56},{8,0},{16,8},{24,16},{32,24},{40,32},{48,40},{56,48},{1,57}... | collective-permute-start | bytes 884744 | tf_op jit(solution)/shard_map/ppermute | solution.py:29
  43.3 6.7 %collective-permute-start.17 = (bf16[128,1152]{1,0:T(8,128)(2,1)S(1)}, bf16[128,1152]{1,0:T(8,128)(2,1)S(1)}, u32[]{:S(2)}, u32[]{:S(2)}) collective-permute-start(bf16[128,1152]{1,0:T(8,128)(2,1)S(1)} %collective-permute-done.12), channel_id=1, source_target_pairs={{0,4},{4,0},{1,5},{5,1},{2,6},{6,2},{3,7},{7,3},{8,12},{12,8},{9,1... | collective-permute-start | bytes 884744 | tf_op jit(solution)/shard_map/ppermute | solution.py:29
  63.2 13.0 %collective-permute-start.21 = (f16[52,32,128]{2,1,0:T(8,128)(2,1)}, f16[52,32,128]{2,1,0:T(8,128)(2,1)}, u32[]{:S(2)}, u32[]{:S(2)}) collective-permute-start(f16[52,32,128]{2,1,0:T(8,128)(2,1)} %get-tuple-element.91), channel_id=1, source_target_pairs={{0,1},{1,2},{2,3},{3,0},{4,5},{5,6},{6,7},{7,4},{8,9},{9,10},{10,1... | collective-permute-start | bytes 1277960 | tf_op jit(solution)/shard_map/ppermute | solution.py:29
  64.6 12.8 %collective-permute-start.23 = (f16[52,32,128]{2,1,0:T(8,128)(2,1)}, f16[52,32,128]{2,1,0:T(8,128)(2,1)}, u32[]{:S(2)}, u32[]{:S(2)}) collective-permute-start(f16[52,32,128]{2,1,0:T(8,128)(2,1)} %get-tuple-element.92), channel_id=1, source_target_pairs={{0,3},{1,0},{2,1},{3,2},{4,7},{5,4},{6,5},{7,6},{8,11},{9,8},{10,9... | collective-permute-start | bytes 1277960 | tf_op jit(solution)/shard_map/ppermute | solution.py:29
  69.5 13.4 %collective-permute-start.22 = (f16[52,32,128]{2,1,0:T(8,128)(2,1)}, f16[52,32,128]{2,1,0:T(8,128)(2,1)S(1)}, u32[]{:S(2)}, u32[]{:S(2)}) collective-permute-start(f16[52,32,128]{2,1,0:T(8,128)(2,1)} %get-tuple-element.93), channel_id=1, source_target_pairs={{0,2},{1,3},{2,0},{3,1},{4,6},{5,7},{6,4},{7,5},{8,10},{9,11},{10,... | collective-permute-start | bytes 1277960 | tf_op jit(solution)/shard_map/ppermute | solution.py:29
  84.2 17.9 %collective-permute-start.26 = (bf16[52,32,128]{2,1,0:T(8,128)(2,1)S(1)}, bf16[52,32,128]{2,1,0:T(8,128)(2,1)S(1)}, u32[]{:S(2)}, u32[]{:S(2)}) collective-permute-start(bf16[52,32,128]{2,1,0:T(8,128)(2,1)S(1)} %fusion.25.refs_0_), channel_id=1, source_target_pairs={{0,1},{1,2},{2,3},{3,0},{4,5},{5,6},{6,7},{7,4},{8,9},{9,10},{10,1... | collective-permute-start | bytes 1277960 | tf_op jit(solution)/shard_map/ppermute | solution.py:29
  85.2 17.0 %collective-permute-start.25 = (bf16[52,32,128]{2,1,0:T(8,128)(2,1)S(1)}, bf16[52,32,128]{2,1,0:T(8,128)(2,1)S(1)}, u32[]{:S(2)}, u32[]{:S(2)}) collective-permute-start(bf16[52,32,128]{2,1,0:T(8,128)(2,1)S(1)} %fusion.25.refs_0_), channel_id=1, source_target_pairs={{0,2},{1,3},{2,0},{3,1},{4,6},{5,7},{6,4},{7,5},{8,10},{9,11},{10,... | collective-permute-start | bytes 1277960 | tf_op jit(solution)/shard_map/ppermute | solution.py:29
  87.8 15.0 %collective-permute-start.24 = (bf16[52,32,128]{2,1,0:T(8,128)(2,1)S(1)}, bf16[52,32,128]{2,1,0:T(8,128)(2,1)S(1)}, u32[]{:S(2)}, u32[]{:S(2)}) collective-permute-start(bf16[52,32,128]{2,1,0:T(8,128)(2,1)S(1)} %fusion.25.refs_0_), channel_id=1, source_target_pairs={{0,3},{1,0},{2,1},{3,2},{4,7},{5,4},{6,5},{7,6},{8,11},{9,8},{10,9... | collective-permute-start | bytes 1277960 | tf_op jit(solution)/shard_map/ppermute | solution.py:29
  113.9 9.4 %collective-permute-start.27 = (bf16[32,32,1152]{2,1,0:T(8,128)(2,1)S(1)}, bf16[32,32,1152]{2,1,0:T(8,128)(2,1)S(1)}, u32[]{:S(2)}, u32[]{:S(2)}) collective-permute-start(bf16[32,32,1152]{2,1,0:T(8,128)(2,1)S(1)} %decode_far.1), channel_id=1, source_target_pairs={{0,64},{64,0},{1,65},{65,1},{2,66},{66,2},{3,67},{67,3},{4,68},{68... | collective-permute-start | bytes 7077896 | tf_op jit(solution)/shard_map/ppermute | solution.py:29
  123.8 17.8 %collective-permute-start.28 = (bf16[8,32,1152]{2,1,0:T(8,128)(2,1)S(1)}, bf16[8,32,1152]{2,1,0:T(8,128)(2,1)S(1)}, u32[]{:S(2)}, u32[]{:S(2)}) collective-permute-start(bf16[8,32,1152]{2,1,0:T(8,128)(2,1)S(1)} %get-tuple-element.88), channel_id=1, source_target_pairs={{0,128},{4,132},{128,0},{132,4},{1,129},{5,133},{129,1},{133,5},{2... | collective-permute-start | bytes 1769480 | tf_op jit(solution)/shard_map/ppermute | solution.py:29
  127.0 26.6 %collective-permute-start.30 = (bf16[8,32,1152]{2,1,0:T(8,128)(2,1)S(1)}, bf16[8,32,1152]{2,1,0:T(8,128)(2,1)S(1)}, u32[]{:S(2)}, u32[]{:S(2)}) collective-permute-start(bf16[8,32,1152]{2,1,0:T(8,128)(2,1)S(1)} %get-tuple-element.89), channel_id=1, source_target_pairs={{0,132},{4,0},{128,4},{132,128},{1,133},{5,1},{129,5},{133,129},{2... | collective-permute-start | bytes 1769480 | tf_op jit(solution)/shard_map/ppermute | solution.py:29
  128.5 26.7 %collective-permute-start.29 = (bf16[8,32,1152]{2,1,0:T(8,128)(2,1)S(1)}, bf16[8,32,1152]{2,1,0:T(8,128)(2,1)S(1)}, u32[]{:S(2)}, u32[]{:S(2)}) collective-permute-start(bf16[8,32,1152]{2,1,0:T(8,128)(2,1)S(1)} %get-tuple-element.90), channel_id=1, source_target_pairs={{0,4},{4,128},{128,132},{132,0},{1,5},{5,129},{129,133},{133,1},{2... | collective-permute-start | bytes 1769480 | tf_op jit(solution)/shard_map/ppermute | solution.py:29
  155.6 14.4 %collective-permute-start.31 = (bf16[32,1152]{1,0:T(8,128)(2,1)S(1)}, bf16[32,1152]{1,0:T(8,128)(2,1)S(1)}, u32[]{:S(2)}, u32[]{:S(2)}) collective-permute-start(bf16[32,1152]{1,0:T(8,128)(2,1)S(1)} %get-tuple-element.94), channel_id=1, source_target_pairs={{0,32},{8,40},{16,48},{24,56},{32,0},{40,8},{48,16},{56,24},{1,33}... | collective-permute-start | bytes 221192 | tf_op jit(solution)/shard_map/ppermute | solution.py:29
  165.1 7.2 %collective-permute-start.37 = (bf16[32,1152]{1,0:T(8,128)(2,1)S(1)}, bf16[32,1152]{1,0:T(8,128)(2,1)S(1)}, u32[]{:S(2)}, u32[]{:S(2)}) collective-permute-start(bf16[32,1152]{1,0:T(8,128)(2,1)S(1)} %get-tuple-element.95), channel_id=1, source_target_pairs={{0,56},{8,0},{16,8},{24,16},{32,24},{40,32},{48,40},{56,48},{1,57}... | collective-permute-start | bytes 221192 | tf_op jit(solution)/shard_map/ppermute | solution.py:29
  165.1 8.8 %collective-permute-start.36 = (bf16[32,1152]{1,0:T(8,128)(2,1)S(1)}, bf16[32,1152]{1,0:T(8,128)(2,1)S(1)}, u32[]{:S(2)}, u32[]{:S(2)}) collective-permute-start(bf16[32,1152]{1,0:T(8,128)(2,1)S(1)} %get-tuple-element.96), channel_id=1, source_target_pairs={{0,8},{8,16},{16,24},{24,32},{32,40},{40,48},{48,56},{56,0},{1,9},... | collective-permute-start | bytes 221192 | tf_op jit(solution)/shard_map/ppermute | solution.py:29
  167.1 6.8 %collective-permute-start.35 = (bf16[32,1152]{1,0:T(8,128)(2,1)S(1)}, bf16[32,1152]{1,0:T(8,128)(2,1)S(1)}, u32[]{:S(2)}, u32[]{:S(2)}) collective-permute-start(bf16[32,1152]{1,0:T(8,128)(2,1)S(1)} %get-tuple-element.97), channel_id=1, source_target_pairs={{0,48},{8,56},{16,0},{24,8},{32,16},{40,24},{48,32},{56,40},{1,49}... | collective-permute-start | bytes 221192 | tf_op jit(solution)/shard_map/ppermute | solution.py:29
  167.1 6.8 %collective-permute-start.34 = (bf16[32,1152]{1,0:T(8,128)(2,1)S(1)}, bf16[32,1152]{1,0:T(8,128)(2,1)S(1)}, u32[]{:S(2)}, u32[]{:S(2)}) collective-permute-start(bf16[32,1152]{1,0:T(8,128)(2,1)S(1)} %get-tuple-element.98), channel_id=1, source_target_pairs={{0,16},{8,24},{16,32},{24,40},{32,48},{40,56},{48,0},{56,8},{1,17}... | collective-permute-start | bytes 221192 | tf_op jit(solution)/shard_map/ppermute | solution.py:29
  170.0 7.8 %collective-permute-start.33 = (bf16[32,1152]{1,0:T(8,128)(2,1)S(1)}, bf16[32,1152]{1,0:T(8,128)(2,1)S(1)}, u32[]{:S(2)}, u32[]{:S(2)}) collective-permute-start(bf16[32,1152]{1,0:T(8,128)(2,1)S(1)} %get-tuple-element.99), channel_id=1, source_target_pairs={{0,40},{8,48},{16,56},{24,0},{32,8},{40,16},{48,24},{56,32},{1,41}... | collective-permute-start | bytes 221192 | tf_op jit(solution)/shard_map/ppermute | solution.py:29
  172.3 8.9 %collective-permute-start.32 = (bf16[32,1152]{1,0:T(8,128)(2,1)S(1)}, bf16[32,1152]{1,0:T(8,128)(2,1)S(1)}, u32[]{:S(2)}, u32[]{:S(2)}) collective-permute-start(bf16[32,1152]{1,0:T(8,128)(2,1)S(1)} %get-tuple-element.100), channel_id=1, source_target_pairs={{0,24},{8,32},{16,40},{24,48},{32,56},{40,0},{48,8},{56,16},{1,25}... | collective-permute-start | bytes 221192 | tf_op jit(solution)/shard_map/ppermute | solution.py:29
  (24 other events, 281.5 us)
where the time goes:
time: 181 us; the launch traced here: 182 us
  waiting for transfers between devices  87.6 us (48%)
  starting transfers between devices  51.4 us (28%)
  Pallas kernels  29.6 us (16%)
  local copies, waits for them, and re-layouts  6.2 us (3%)
  other arithmetic  5.63 us (3%)
    ppermute x32, waiting for transfers between devices, shift(): return lambda value: lax.ppermute(value, axis, pairs)  87.6 us
    ppermute x32, starting transfers between devices, shift(): return lambda value: lax.ppermute(value, axis, pairs)  51.4 us
    pallas_call x2, Pallas kernels, decode(): pl.pallas_call(functools.partial(decode_kernel, near), out_shape=jax.Shap...  17.9 us
    pallas_call x1, Pallas kernels, encode(): pl.pallas_call(functools.partial(encode_kernel, low, high), out_shape=jax...  11.7 us
  transfers between devices with their start and end apart: 32, of which 17 were waited for; matrix products, arithmetic and copies ran while one was open for 3% of the time, Pallas kernels for 5%

commit v1 on v0

v1 whole, which is shorter than its diff:
```python
import functools

import jax
import jax.numpy as jnp
from jax import lax
from jax.experimental import pallas as pl
from jax.experimental.pallas import tpu as pltpu
from jax.sharding import Mesh, PartitionSpec as P

BLOCK = 128
BPO = 16
TILE = 32
TILES = 64
WIDTH = 1152
LATENTS = BPO * BLOCK
SLOTS = 320
FAST = 208
EARLY = 10
GROUP = 8
UNROLL = 4
SCALE = 16.0
F32 = jnp.float32
BF16 = jnp.bfloat16
Y = ("yh", "yl")
Y_WAYS = (2, 1, 3)


def shift(axis, step, size):
    pairs = [(i, (i + step) % size) for i in range(size)]
    return lambda value: lax.ppermute(value, axis, pairs)


ARRIVALS = (
    (0, 0), (0, 1), (0, -1), (0, 2), (0, -2), (0, 3), (0, -3), (1, 0), (1, -1), (1, 1),
    (0, 4), (1, 2), (1, -2), (1, 3), (1, -3), (1, 4),
)


def gather_tokens(rows):
    up, down, swap = shift("z", 1, 8), shift("z", -1, 8), shift("yl", 1, 2)
    own, other = {0: rows}, {}
    own[-1], own[1], other[0] = up(own[0]), down(own[0]), swap(own[0])
    own[-2], own[2], other[-1] = up(own[-1]), down(own[1]), swap(own[-1])
    own[-3], own[3], other[1] = up(own[-2]), down(own[2]), swap(own[1])
    own[4], other[2], other[-2] = up(own[-3]), down(other[1]), swap(own[-2])
    other[-3], other[3], other[4] = up(other[-2]), down(other[2]), swap(own[4])
    return [(own, other)[column][distance] for column, distance in ARRIVALS]


def make_table(lists, places):
    y = places["yh"] * 2 + places["yl"]
    tok = places["z"] * 2 + places["yl"]
    block = jnp.arange(BPO, dtype=jnp.int32)
    tile = jnp.arange(TILES, dtype=jnp.int32)
    column = ((tile >> 2) & 1) ^ places["yl"]
    distance = ((tile >> 3) - places["z"]) & 7
    shard = sum(
        jnp.where((column == c) & (distance == d % 8), i, 0) for i, (c, d) in enumerate(ARRIVALS)
    )
    source = shard * 4 + (tile & 3)
    named = jnp.any(lists[None] == (tok * BPO + block)[:, None, None], axis=2)
    before = jnp.dot(named.astype(F32), (source[:, None] < source[None, :]).astype(F32))
    counts = jnp.sum(named.astype(jnp.int32), axis=1)
    early = jnp.sum((named & (source < 4 * EARLY)[None, :]).astype(jnp.int32), axis=1)
    ends = jnp.sum(jnp.where(block[None, :] <= block[:, None], counts[None, :], 0), axis=1)
    starts = ends - counts
    rank = jnp.where(named, before.astype(jnp.int32) + starts[:, None], -1)
    far = ((tile >> 4) & 1) ^ places["core"]
    target = (1 - far) * 32 + ((((tile >> 5) * 2 + (tile & 1)) - y) & 3) * 8 + ((tile >> 1) & 7)
    code = (source + 1024 * target)[None, :] + 64 * block[:, None]
    slot = jnp.arange(SLOTS, dtype=jnp.int32)
    hit = rank.reshape(1, -1) == slot[:, None]
    found = jnp.sum(jnp.where(hit, code.reshape(1, -1), 0), axis=1)
    row = jnp.where(slot < FAST, turned(slot, 0, FAST, places), turned(slot, FAST, SLOTS, places))
    facts = jnp.concatenate([starts, starts + early, ends, jnp.stack([ends[BPO - 1], places["x"]])])
    return found + 65536 * row, facts


def turned(slot, low, high, places):
    part = (high - low) // 4
    quarter = (slot - low) // part
    return low + ((quarter - places["x"]) & 3) * part + slot - low - quarter * part


def encode_kernel(count, lead, bounds, low, high, table, facts, *refs):
    shards, w_ref, refs = refs[:count], refs[count], refs[count + 1 :]
    earlier, (out_ref, rows, lhs, sem, back_sem) = refs[:-5], refs[-5:]
    copies = [pltpu.make_async_copy(s, rows.at[pl.ds(4 * i, 4)], sem.at[i]) for i, s in enumerate(shards)]
    copies += [pltpu.make_async_copy(e, out_ref, back_sem) for e in earlier]
    for c in copies:
        c.start()
    for c in copies:
        c.wait()

    def block(index, carry):
        first = jnp.maximum(facts[bounds[0] * BPO + index], low)
        last = jnp.minimum(facts[bounds[1] * BPO + index], high)
        column = pl.ds(pl.multiple_of(index * BLOCK, BLOCK), BLOCK)

        def group(g, carry):
            codes = [table[jnp.minimum(first + g * GROUP + u, last - 1)] for u in range(GROUP)]
            for u in range(GROUP):
                lhs[pl.ds(u * TILE, TILE), :] = rows[(codes[u] & 63) - 4 * lead]
            part = jnp.dot(lhs[...], w_ref[:, column], preferred_element_type=F32)
            for u in range(GROUP):
                out_ref[(codes[u] >> 16) - low] = part[u * TILE : (u + 1) * TILE]
            return carry

        return lax.fori_loop(0, (jnp.maximum(last - first, 0) + GROUP - 1) // GROUP, group, carry)

    lax.fori_loop(0, BPO, block, 0)


def encode(lead, bounds, low, high, table, facts, shards, w_enc, *earlier):
    count = len(shards)
    any_space = pl.BlockSpec(memory_space=pl.ANY)
    vmem = pl.BlockSpec(memory_space=pltpu.VMEM)
    return pl.pallas_call(
        functools.partial(encode_kernel, count, lead, bounds, low, high),
        out_shape=jax.ShapeDtypeStruct((high - low, TILE, BLOCK), F32),
        grid_spec=pltpu.PrefetchScalarGridSpec(
            num_scalar_prefetch=2,
            grid=(),
            in_specs=[any_space] * count + [vmem] + [any_space] * len(earlier),
            out_specs=vmem,
            scratch_shapes=[
                pltpu.VMEM((4 * count, TILE, WIDTH), BF16),
                pltpu.VMEM((GROUP * TILE, WIDTH), BF16),
                pltpu.SemaphoreType.DMA((count,)),
                pltpu.SemaphoreType.DMA,
            ],
        ),
        compiler_params=pltpu.CompilerParams(vmem_limit_bytes=20 << 20),
        cost_estimate=pl.CostEstimate(flops=count * 5 * 10**8, bytes_accessed=4 * 10**6, transcendentals=0),
        name="encode",
    )(table, facts, *[s.reshape(4, TILE, WIDTH) for s in shards], w_enc, *earlier)


def place_kernel(table, facts, *refs):
    pieces, dense = refs[:5], refs[5]
    dense[...] = jnp.zeros_like(dense)
    total, x = facts[3 * BPO], facts[3 * BPO + 1]
    part = FAST // 4
    for i, piece in enumerate(pieces):
        if i < 4:
            first = ((x + i) & 3) * part
            last = jnp.minimum(first + part, total)
        else:
            first, last = FAST, total

        def move(g, carry, i=i, piece=piece, first=first, last=last):
            for u in range(UNROLL):
                slot = jnp.minimum(first + g * UNROLL + u, last - 1)
                code = table[slot]
                line = pl.ds(pl.multiple_of(((code >> 10) & 63) * TILE, TILE), TILE)
                lane = pl.ds(pl.multiple_of(((code >> 6) & 15) * BLOCK, BLOCK), BLOCK)
                dense[line, lane] = piece[slot - first if i < 4 else (code >> 16) - FAST]
            return carry

        lax.fori_loop(0, (jnp.maximum(last - first, 0) + UNROLL - 1) // UNROLL, move, 0)


def place(table, facts, pieces):
    vmem = pl.BlockSpec(memory_space=pltpu.VMEM)
    return pl.pallas_call(
        place_kernel,
        out_shape=jax.ShapeDtypeStruct((TILES * TILE, LATENTS), BF16),
        grid_spec=pltpu.PrefetchScalarGridSpec(
            num_scalar_prefetch=2, grid=(), in_specs=[vmem] * 5, out_specs=vmem
        ),
        compiler_params=pltpu.CompilerParams(vmem_limit_bytes=16 << 20),
        cost_estimate=pl.CostEstimate(flops=10**6, bytes_accessed=8 * 10**6, transcendentals=0),
        name="place",
    )(table, facts, *pieces)


def activate(low, high, pre, table, thresholds, places):
    right, left, across = shift("x", 1, 4), shift("x", -1, 4), shift("x", 2, 4)
    part = (high - low) // 4
    quarters = [pre[r * part : (r + 1) * part] for r in range(4)]
    sent = [(q * SCALE).astype(jnp.float16) for q in quarters[1:]]
    got = [right(sent[0]), across(sent[1]), left(sent[2])]
    block = (lax.dynamic_slice(table, (low + places["x"] * part,), (part,)) >> 6) & 15
    pick = (block[:, None] == jnp.arange(BPO, dtype=jnp.int32)[None, :]).astype(F32)
    limits = jnp.dot(pick, thresholds.astype(F32) * 0.125, precision=lax.Precision.HIGHEST)
    summed = quarters[0] + (got[0].astype(F32) + got[1].astype(F32) + got[2].astype(F32)) * (1.0 / SCALE)
    acts = jnp.maximum(summed - limits[:, None, :], 0.0).astype(BF16)
    return acts, left(acts), across(acts), right(acts)


def some_more(table, facts, thresholds, w_enc, places, *shards):
    pre = encode(0, (0, 2), FAST, SLOTS, table, facts, shards, w_enc)
    return jnp.concatenate(activate(FAST, SLOTS, pre, table, thresholds, places))


def no_more(table, facts, thresholds, w_enc, places, *shards):
    return jnp.zeros((SLOTS - FAST, TILE, BLOCK), BF16)


def reduce_tokens(mine, other):
    mine = mine.reshape(4, 8, TILE, WIDTH)
    other = other.reshape(4, 8, TILE, WIDTH)
    got = [shift(Y, r, 4)((mine[r] + other[r].astype(F32)).astype(BF16)) for r in Y_WAYS]
    column = mine[0] + other[0].astype(F32) + got[0].astype(F32) + got[1].astype(F32) + got[2].astype(F32)
    got = lax.all_to_all(column.astype(BF16), "z", 0, 0, tiled=True)
    return jnp.sum(got.astype(F32), axis=0).astype(BF16)


def shards(resid, block_lists, threshold_level, w_enc, w_dec):
    places = {name: lax.axis_index(name) for name in ("yh", "core", "z", "yl", "x")}
    w_enc, w_dec = w_enc[0], w_dec[0]
    thresholds = threshold_level[0].reshape(BPO, BLOCK)
    table, facts = make_table(block_lists[0], places)
    gathered = gather_tokens(resid[0])
    if EARLY:
        pre = encode(0, (0, 1), 0, FAST, table, facts, gathered[:EARLY], w_enc)
        pre = encode(EARLY, (1, 2), 0, FAST, table, facts, gathered[EARLY:], w_enc, pre)
    else:
        pre = encode(0, (0, 2), 0, FAST, table, facts, gathered, w_enc)
    pieces = activate(0, FAST, pre, table, thresholds, places)
    more = lax.cond(facts[3 * BPO] > FAST, some_more, no_more, table, facts, thresholds, w_enc, places, *gathered)
    acts = place(table, facts, pieces + (more,))
    half = TILES * TILE // 2
    theirs = jnp.dot(acts[:half], w_dec, preferred_element_type=F32).astype(BF16)
    other = shift("core", 1, 2)(theirs)
    acts, theirs = lax.optimization_barrier((acts, theirs))
    mine = jnp.dot(acts[half:], w_dec, preferred_element_type=F32)
    return reduce_tokens(mine, other)


def solution(mesh):
    section, tok, lat = ("yh", "core"), ("z", "yl"), "x"
    fine = Mesh(mesh.devices.reshape(2, 2, 8, 2, 4), section + tok + (lat,))
    return jax.shard_map(
        shards,
        mesh=fine,
        in_specs=(
            P(section, tok, lat),
            P(section, None, None),
            P(section, tok),
            P(section, lat, tok),
            P(section, tok, lat),
        ),
        out_specs=P(section + tok, lat),
        check_vma=False,
    )
```

time: 181 us -> 173 us (0.956); the launches traced: 182 us -> 172 us
  blocking collectives: 0 us -> 24.5 us
  starting transfers between devices: 51.4 us -> 34.7 us
  waiting for transfers between devices: 87.6 us -> 70.9 us
  matrix products: 0.41 us -> 11.7 us
  Pallas kernels: 29.6 us -> 20.3 us
  local copies, waits for them, and re-layouts: 6.2 us -> 2.62 us
    all_to_all x0 -> x1, blocking collectives: none -> 24.5 us  [reduce_tokens(): got = lax.all_to_all(column.astype(BF16), 'z', 0, 0, tiled=True)]
    ppermute x32 -> x25, waiting for transfers between devices: 87.6 us -> 70.9 us  [shift(): return lambda value: lax.ppermute(value, axis, pairs)]
    ppermute x32 -> x25, starting transfers between devices: 51.4 us -> 34.7 us  [shift(): return lambda value: lax.ppermute(value, axis, pairs)]
    dot_general x1 -> x3, matrix products: 0.19 us -> 11.5 us  [the longest x1 5.77 us: shards(): jnp.dot(acts[:half], w_dec, preferred_element_type=F32).astype(BF16)]
    pallas_call x3, Pallas kernels: 29.6 us -> 20.3 us  [the longest x2 18.1 us: encode(): pl.pallas_call(functools.partial(encode_kernel, count, lead, bounds, low,...]
    unnamed x48 -> x32, local copies, waits for them, and re-layouts: 2.44 us -> 0.07 us
    another operation x5 -> x1, local copies, waits for them, and re-layouts: 2.95 us -> 1.06 us
  transfers between devices with their start and end apart: 32 -> 25, of which waited for: 17 -> 11; matrix products, arithmetic and copies ran while one was open for 3% -> 6% of each run, Pallas kernels for 5% -> 6%
where the time goes in v1:
time: 173 us; the launch traced here: 172 us
  waiting for transfers between devices  70.9 us (41%)
  starting transfers between devices  34.7 us (20%)
  blocking collectives  24.5 us (14%)
  Pallas kernels  20.3 us (12%)
  matrix products  11.7 us (7%)
  other arithmetic  5.84 us (3%)
  local copies, waits for them, and re-layouts  2.62 us (2%)
    ppermute x25, waiting for transfers between devices, shift(): return lambda value: lax.ppermute(value, axis, pairs)  70.9 us
    ppermute x25, starting transfers between devices, shift(): return lambda value: lax.ppermute(value, axis, pairs)  34.7 us
    all_to_all x1, blocking collectives, reduce_tokens(): got = lax.all_to_all(column.astype(BF16), 'z', 0, 0, tiled=True)  24.5 us
    pallas_call x2, Pallas kernels, encode(): pl.pallas_call(functools.partial(encode_kernel, count, lead, bounds, low,...  18.1 us
    dot_general x1, matrix products, shards(): jnp.dot(acts[:half], w_dec, preferred_element_type=F32).astype(BF16)  5.77 us
    dot_general x1, matrix products, shards(): mine = jnp.dot(acts[half:], w_dec, preferred_element_type=F32)  5.56 us
  transfers between devices with their start and end apart: 25, of which 11 were waited for; matrix products, arithmetic and copies ran while one was open for 6% of the time, Pallas kernels for 6%

profile of v1, /device:TPU:8, one launch (start us, length us, event | category | flops | bytes accessed | tf_op | source)
XLA Modules:
  0.0 171.5 jit_solution(4971756840487210375)
XLA Ops:
  0.0 2.2 %collective-permute-start.19 = (bf16[128,1152]{1,0:T(8,128)(2,1)}, bf16[128,1152]{1,0:T(8,128)(2,1)S(1)}, u32[]{:S(2)}, u32[]{:S(2)}) collective-permute-start(bf16[128,1152]{1,0:T(8,128)(2,1)} %bitcast.72), channel_id=1, source_target_pairs={{0,4},{4,0},{1,5},{5,1},{2,6},{6,2},{3,7},{7,3},{8,12},{12,8},{9,1... | collective-permute-start | bytes 884744 | tf_op jit(solution)/shard_map/ppermute | solution.py:30
  2.2 4.1 %collective-permute-start.10 = (bf16[128,1152]{1,0:T(8,128)(2,1)}, bf16[128,1152]{1,0:T(8,128)(2,1)S(1)}, u32[]{:S(2)}, u32[]{:S(2)}) collective-permute-start(bf16[128,1152]{1,0:T(8,128)(2,1)} %bitcast.73), channel_id=1, source_target_pairs={{0,56},{8,0},{16,8},{24,16},{32,24},{40,32},{48,40},{56,48},{1,57}... | collective-permute-start | bytes 884744 | tf_op jit(solution)/shard_map/ppermute | solution.py:30
  7.4 8.5 %collective-permute-done.6 = bf16[128,1152]{1,0:T(8,128)(2,1)S(1)} collective-permute-done((bf16[128,1152]{1,0:T(8,128)(2,1)}, bf16[128,1152]{1,0:T(8,128)(2,1)S(1)}, u32[]{:S(2)}, u32[]{:S(2)}) %collective-permute-start.6) | collective-permute-done | bytes 294944 | tf_op jit(solution)/shard_map/ppermute | solution.py:30
  16.2 3.3 %collective-permute-start.17 = (bf16[128,1152]{1,0:T(8,128)(2,1)S(1)}, bf16[128,1152]{1,0:T(8,128)(2,1)S(1)}, u32[]{:S(2)}, u32[]{:S(2)}) collective-permute-start(bf16[128,1152]{1,0:T(8,128)(2,1)S(1)} %collective-permute-done.10), channel_id=1, source_target_pairs={{0,56},{8,0},{16,8},{24,16},{32,24},{40,32},{48,40},{56,48},{1,57}... | collective-permute-start | bytes 884744 | tf_op jit(solution)/shard_map/ppermute | solution.py:30
  19.5 1.6 collective-permute-start.11
  21.1 3.3 %collective-permute-done.7 = bf16[128,1152]{1,0:T(8,128)(2,1)S(1)} collective-permute-done((bf16[128,1152]{1,0:T(8,128)(2,1)S(1)}, bf16[128,1152]{1,0:T(8,128)(2,1)S(1)}, u32[]{:S(2)}, u32[]{:S(2)}) %collective-permute-start.7) | collective-permute-done | bytes 294944 | tf_op jit(solution)/shard_map/ppermute | solution.py:30
  24.5 1.6 collective-permute-start.20
  26.6 3.2 %collective-permute-start.18 = (bf16[128,1152]{1,0:T(8,128)(2,1)S(1)}, bf16[128,1152]{1,0:T(8,128)(2,1)}, u32[]{:S(2)}, u32[]{:S(2)}) collective-permute-start(bf16[128,1152]{1,0:T(8,128)(2,1)S(1)} %collective-permute-done.17), channel_id=1, source_target_pairs={{0,56},{8,0},{16,8},{24,16},{32,24},{40,32},{48,40},{56,48},{1,57}... | collective-permute-start | bytes 884744 | tf_op jit(solution)/shard_map/ppermute | solution.py:30
  29.9 2.4 %collective-permute-done.8 = bf16[128,1152]{1,0:T(8,128)(2,1)S(1)} collective-permute-done((bf16[128,1152]{1,0:T(8,128)(2,1)S(1)}, bf16[128,1152]{1,0:T(8,128)(2,1)S(1)}, u32[]{:S(2)}, u32[]{:S(2)}) %collective-permute-start.8) | collective-permute-done | bytes 294944 | tf_op jit(solution)/shard_map/ppermute | solution.py:30
  34.6 5.3 %collective-permute-done.12 = bf16[128,1152]{1,0:T(8,128)(2,1)S(1)} collective-permute-done((bf16[128,1152]{1,0:T(8,128)(2,1)S(1)}, bf16[128,1152]{1,0:T(8,128)(2,1)S(1)}, u32[]{:S(2)}, u32[]{:S(2)}) %collective-permute-start.12) | collective-permute-done | bytes 294944 | tf_op jit(solution)/shard_map/ppermute | solution.py:30
  39.9 3.3 %collective-permute-start.14 = (bf16[128,1152]{1,0:T(8,128)(2,1)S(1)}, bf16[128,1152]{1,0:T(8,128)(2,1)S(1)}, u32[]{:S(2)}, u32[]{:S(2)}) collective-permute-start(bf16[128,1152]{1,0:T(8,128)(2,1)S(1)} %collective-permute-done.12), channel_id=1, source_target_pairs={{0,56},{8,0},{16,8},{24,16},{32,24},{40,32},{48,40},{56,48},{1,57}... | collective-permute-start | bytes 884744 | tf_op jit(solution)/shard_map/ppermute | solution.py:30
  43.2 1.8 %collective-permute-start.16 = (bf16[128,1152]{1,0:T(8,128)(2,1)S(1)}, bf16[128,1152]{1,0:T(8,128)(2,1)S(1)}, u32[]{:S(2)}, u32[]{:S(2)}) collective-permute-start(bf16[128,1152]{1,0:T(8,128)(2,1)S(1)} %collective-permute-done.9), channel_id=1, source_target_pairs={{0,4},{4,0},{1,5},{5,1},{2,6},{6,2},{3,7},{7,3},{8,12},{12,8},{9,1... | collective-permute-start | bytes 884744 | tf_op jit(solution)/shard_map/ppermute | solution.py:30
  45.1 10.9 %encode.4.refs_7_ = f32[208,32,128]{2,1,0:T(8,128)S(1)} custom-call(s32[320]{0:T(512)S(1)} %multiply_add_fusion.table, s32[50]{0:T(128)S(1)} %concatenate.6.facts, bf16[4,32,1152]{2,1,0:T(8,128)(2,1)} %bitcast.75, bf16[4,32,1152]{2,1,0:T(8,128)(2,1)S(1)} %bitcast.79, bf16[4,32,1152]{2,1,0:T(8,128)(2,1)S(1)} %bitcast.81, bf16[4,32,1152]{2,1,0:T(8,128)(2,1)S(1)} %bitcast.85, ...), custom_call_target="tpu_custom_call" | custom-call | flops 5000000000 | bytes 4000000 | tf_op jit(solution)/shard_map/encode/pallas_call | solution.py:118
  56.2 7.2 %encode.5 = f32[208,32,128]{2,1,0:T(8,128)S(1)} custom-call(s32[320]{0:T(512)S(1)} %multiply_add_fusion.table, s32[50]{0:T(128)S(1)} %concatenate.6.facts, bf16[4,32,1152]{2,1,0:T(8,128)(2,1)} %bitcast.61, bf16[4,32,1152]{2,1,0:T(8,128)(2,1)} %bitcast.59, bf16[4,32,1152]{2,1,0:T(8,128)(2,1)} %bitcast.57, bf16[4,32,1152]{2,1,0:T(8,128)(2,1)S(1)} %bitcast.63, ...), custom_call_target="tpu_custom_call" | custom-call | flops 3000000000 | bytes 4000000 | tf_op jit(solution)/shard_map/encode/pallas_call | solution.py:118
  63.4 1.2 fusion.30
  64.6 1.5 collective-permute-start.21
  66.1 1.7 %collective-permute-start.23 = (f16[52,32,128]{2,1,0:T(8,128)(2,1)}, f16[52,32,128]{2,1,0:T(8,128)(2,1)}, u32[]{:S(2)}, u32[]{:S(2)}) collective-permute-start(f16[52,32,128]{2,1,0:T(8,128)(2,1)} %get-tuple-element.87), channel_id=1, source_target_pairs={{0,3},{1,0},{2,1},{3,2},{4,7},{5,4},{6,5},{7,6},{8,11},{9,8},{10,9... | collective-permute-start | bytes 1277960 | tf_op jit(solution)/shard_map/ppermute | solution.py:30
  67.8 1.1 conditional.1
  68.9 1.8 %collective-permute-start.22 = (f16[52,32,128]{2,1,0:T(8,128)(2,1)}, f16[52,32,128]{2,1,0:T(8,128)(2,1)}, u32[]{:S(2)}, u32[]{:S(2)}) collective-permute-start(f16[52,32,128]{2,1,0:T(8,128)(2,1)} %get-tuple-element.88), channel_id=1, source_target_pairs={{0,2},{1,3},{2,0},{3,1},{4,6},{5,7},{6,4},{7,5},{8,10},{9,11},{10,... | collective-permute-start | bytes 1277960 | tf_op jit(solution)/shard_map/ppermute | solution.py:30
  71.0 7.6 %collective-permute-done.21 = f16[52,32,128]{2,1,0:T(8,128)(2,1)} collective-permute-done((f16[52,32,128]{2,1,0:T(8,128)(2,1)}, f16[52,32,128]{2,1,0:T(8,128)(2,1)}, u32[]{:S(2)}, u32[]{:S(2)}) %collective-permute-start.21) | collective-permute-done | bytes 426016 | tf_op jit(solution)/shard_map/ppermute | solution.py:30
  78.6 5.1 %collective-permute-done.22 = f16[52,32,128]{2,1,0:T(8,128)(2,1)} collective-permute-done((f16[52,32,128]{2,1,0:T(8,128)(2,1)}, f16[52,32,128]{2,1,0:T(8,128)(2,1)}, u32[]{:S(2)}, u32[]{:S(2)}) %collective-permute-start.22) | collective-permute-done | bytes 426016 | tf_op jit(solution)/shard_map/ppermute | solution.py:30
  83.7 1.7 fusion.33.refs_0_
  86.2 2.2 %collective-permute-start.25 = (bf16[52,32,128]{2,1,0:T(8,128)(2,1)S(1)}, bf16[52,32,128]{2,1,0:T(8,128)(2,1)S(1)}, u32[]{:S(2)}, u32[]{:S(2)}) collective-permute-start(bf16[52,32,128]{2,1,0:T(8,128)(2,1)S(1)} %fusion.33.refs_0_), channel_id=1, source_target_pairs={{0,2},{1,3},{2,0},{3,1},{4,6},{5,7},{6,4},{7,5},{8,10},{9,11},{10,... | collective-permute-start | bytes 1277960 | tf_op jit(solution)/shard_map/ppermute | solution.py:30
  89.0 12.5 %collective-permute-done.26.refs_3_ = bf16[52,32,128]{2,1,0:T(8,128)(2,1)S(1)} collective-permute-done((bf16[52,32,128]{2,1,0:T(8,128)(2,1)S(1)}, bf16[52,32,128]{2,1,0:T(8,128)(2,1)S(1)}, u32[]{:S(2)}, u32[]{:S(2)}) %collective-permute-start.26) | collective-permute-done | bytes 426016 | tf_op jit(solution)/shard_map/ppermute | solution.py:30
  101.6 2.2 %place.1 = bf16[2048,2048]{1,0:T(8,128)(2,1)S(1)} custom-call(s32[320]{0:T(512)S(1)} %multiply_add_fusion.table, s32[50]{0:T(128)S(1)} %concatenate.6.facts, bf16[52,32,128]{2,1,0:T(8,128)(2,1)S(1)} %fusion.33.refs_0_, bf16[52,32,128]{2,1,0:T(8,128)(2,1)S(1)} %collective-permute-done.24.refs_1_, bf16[52,32,128]{2,1,0:T(8,128)(2,1)S(1)} %collective-permute-done.25.refs_2_, ...), custom_call_target="tpu_custom_call" | custom-call | flops 1000000 | bytes 8000000 | tf_op jit(solution)/shard_map/place/pallas_call | solution.py:165
  103.9 5.8 %fusion.18 = bf16[1024,1152]{1,0:T(8,128)(2,1)S(1)} fusion(bf16[1,2048,1152]{2,1,0:T(8,128)(2,1)S(1)} %bitcast.71, bf16[2048,2048]{1,0:T(8,128)(2,1)S(1)} %place.1), kind=kOutput, calls=%fused_computation.25 | convolution fusion | flops 4833017856 | bytes 11272192 | tf_op jit(solution)/shard_map/dot_general | solution.py:224
  109.8 5.6 %fusion.12 = f32[1024,1152]{1,0:T(8,128)S(1)} fusion(bf16[1,2048,1152]{2,1,0:T(8,128)(2,1)S(1)} %bitcast.71, bf16[2048,2048]{1,0:T(8,128)(2,1)S(1)} %place.1), kind=kOutput, calls=%fused_computation.19 | convolution fusion | flops 4831838208 | bytes 13631488 | tf_op jit(solution)/shard_map/dot_general | solution.py:227
  115.8 1.8 %collective-permute-start.30 = (bf16[8,32,1152]{2,1,0:T(8,128)(2,1)S(1)}, bf16[8,32,1152]{2,1,0:T(8,128)(2,1)S(1)}, u32[]{:S(2)}, u32[]{:S(2)}) collective-permute-start(bf16[8,32,1152]{2,1,0:T(8,128)(2,1)S(1)} %bitcast.56), channel_id=1, source_target_pairs={{0,132},{4,0},{128,4},{132,128},{1,133},{5,1},{129,5},{133,129},{2... | collective-permute-start | bytes 1769480 | tf_op jit(solution)/shard_map/ppermute | solution.py:30
  118.7 1.4 collective-permute-start.29
  120.0 11.6 %collective-permute-done.30 = bf16[8,32,1152]{2,1,0:T(8,128)(2,1)S(1)} collective-permute-done((bf16[8,32,1152]{2,1,0:T(8,128)(2,1)S(1)}, bf16[8,32,1152]{2,1,0:T(8,128)(2,1)S(1)}, u32[]{:S(2)}, u32[]{:S(2)}) %collective-permute-start.30) | collective-permute-done | bytes 589856 | tf_op jit(solution)/shard_map/ppermute | solution.py:30
  131.6 13.4 %collective-permute-done.28 = bf16[8,32,1152]{2,1,0:T(8,128)(2,1)S(1)} collective-permute-done((bf16[8,32,1152]{2,1,0:T(8,128)(2,1)S(1)}, bf16[8,32,1152]{2,1,0:T(8,128)(2,1)S(1)}, u32[]{:S(2)}, u32[]{:S(2)}) %collective-permute-start.28) | collective-permute-done | bytes 589856 | tf_op jit(solution)/shard_map/ppermute | solution.py:30
  146.3 24.5 %all_to_all.5 = bf16[8,32,1152]{2,1,0:T(8,128)(2,1)S(1)} all-to-all(bf16[8,32,1152]{2,1,0:T(8,128)(2,1)S(1)} %add_convert_fusion), channel_id=1, replica_groups=mesh['yh'=2,'core'=2,'z'=8,'yl'=2,'x'=4] {'z'}, dimensions={0} | all-to-all | bytes 1179648 | tf_op jit(solution)/shard_map/all_to_all | solution.py:205
  (82 shorter events, 10.4 us)
Async XLA Ops:
  0.0 26.1 %collective-permute-start.19 = (bf16[128,1152]{1,0:T(8,128)(2,1)}, bf16[128,1152]{1,0:T(8,128)(2,1)S(1)}, u32[]{:S(2)}, u32[]{:S(2)}) collective-permute-start(bf16[128,1152]{1,0:T(8,128)(2,1)} %bitcast.72), channel_id=1, source_target_pairs={{0,4},{4,0},{1,5},{5,1},{2,6},{6,2},{3,7},{7,3},{8,12},{12,8},{9,1... | collective-permute-start | bytes 884744 | tf_op jit(solution)/shard_map/ppermute | solution.py:30
  2.2 14.0 %collective-permute-start.10 = (bf16[128,1152]{1,0:T(8,128)(2,1)}, bf16[128,1152]{1,0:T(8,128)(2,1)S(1)}, u32[]{:S(2)}, u32[]{:S(2)}) collective-permute-start(bf16[128,1152]{1,0:T(8,128)(2,1)} %bitcast.73), channel_id=1, source_target_pairs={{0,56},{8,0},{16,8},{24,16},{32,24},{40,32},{48,40},{56,48},{1,57}... | collective-permute-start | bytes 884744 | tf_op jit(solution)/shard_map/ppermute | solution.py:30
  6.3 9.6 %collective-permute-start.6 = (bf16[128,1152]{1,0:T(8,128)(2,1)}, bf16[128,1152]{1,0:T(8,128)(2,1)S(1)}, u32[]{:S(2)}, u32[]{:S(2)}) collective-permute-start(bf16[128,1152]{1,0:T(8,128)(2,1)} %bitcast.74), channel_id=1, source_target_pairs={{0,8},{8,16},{16,24},{24,32},{32,40},{40,48},{48,56},{56,0},{1,9},... | collective-permute-start | bytes 884744 | tf_op jit(solution)/shard_map/ppermute | solution.py:30
  15.9 40.1 %copy-start.8 = (bf16[128,1152]{1,0:T(8,128)(2,1)}, bf16[128,1152]{1,0:T(8,128)(2,1)S(1)}, u32[]{:S(2)}) copy-start(bf16[128,1152]{1,0:T(8,128)(2,1)S(1)} %collective-permute-done.6) | copy-start | bytes 884740
  15.9 8.5 %collective-permute-start.7 = (bf16[128,1152]{1,0:T(8,128)(2,1)S(1)}, bf16[128,1152]{1,0:T(8,128)(2,1)S(1)}, u32[]{:S(2)}, u32[]{:S(2)}) collective-permute-start(bf16[128,1152]{1,0:T(8,128)(2,1)S(1)} %collective-permute-done.6), channel_id=1, source_target_pairs={{0,8},{8,16},{16,24},{24,32},{32,40},{40,48},{48,56},{56,0},{1,9},... | collective-permute-start | bytes 884744 | tf_op jit(solution)/shard_map/ppermute | solution.py:30
  16.2 39.9 %copy-start.7 = (bf16[128,1152]{1,0:T(8,128)(2,1)}, bf16[128,1152]{1,0:T(8,128)(2,1)S(1)}, u32[]{:S(2)}) copy-start(bf16[128,1152]{1,0:T(8,128)(2,1)S(1)} %collective-permute-done.10) | copy-start | bytes 884740
  16.2 10.4 %collective-permute-start.17 = (bf16[128,1152]{1,0:T(8,128)(2,1)S(1)}, bf16[128,1152]{1,0:T(8,128)(2,1)S(1)}, u32[]{:S(2)}, u32[]{:S(2)}) collective-permute-start(bf16[128,1152]{1,0:T(8,128)(2,1)S(1)} %collective-permute-done.10), channel_id=1, source_target_pairs={{0,56},{8,0},{16,8},{24,16},{32,24},{40,32},{48,40},{56,48},{1,57}... | collective-permute-start | bytes 884744 | tf_op jit(solution)/shard_map/ppermute | solution.py:30
  19.5 10.3 %collective-permute-start.11 = (bf16[128,1152]{1,0:T(8,128)(2,1)S(1)}, bf16[128,1152]{1,0:T(8,128)(2,1)S(1)}, u32[]{:S(2)}, u32[]{:S(2)}) collective-permute-start(bf16[128,1152]{1,0:T(8,128)(2,1)S(1)} %collective-permute-done.10), channel_id=1, source_target_pairs={{0,4},{4,0},{1,5},{5,1},{2,6},{6,2},{3,7},{7,3},{8,12},{12,8},{9,1... | collective-permute-start | bytes 884744 | tf_op jit(solution)/shard_map/ppermute | solution.py:30
  24.4 31.7 %copy-start.9 = (bf16[128,1152]{1,0:T(8,128)(2,1)}, bf16[128,1152]{1,0:T(8,128)(2,1)S(1)}, u32[]{:S(2)}) copy-start(bf16[128,1152]{1,0:T(8,128)(2,1)S(1)} %collective-permute-done.7) | copy-start | bytes 884740
  24.4 7.9 %collective-permute-start.8 = (bf16[128,1152]{1,0:T(8,128)(2,1)S(1)}, bf16[128,1152]{1,0:T(8,128)(2,1)S(1)}, u32[]{:S(2)}, u32[]{:S(2)}) collective-permute-start(bf16[128,1152]{1,0:T(8,128)(2,1)S(1)} %collective-permute-done.7), channel_id=1, source_target_pairs={{0,8},{8,16},{16,24},{24,32},{32,40},{40,48},{48,56},{56,0},{1,9},... | collective-permute-start | bytes 884744 | tf_op jit(solution)/shard_map/ppermute | solution.py:30
  24.5 20.5 %collective-permute-start.20 = (bf16[128,1152]{1,0:T(8,128)(2,1)S(1)}, bf16[128,1152]{1,0:T(8,128)(2,1)S(1)}, u32[]{:S(2)}, u32[]{:S(2)}) collective-permute-start(bf16[128,1152]{1,0:T(8,128)(2,1)S(1)} %collective-permute-done.6), channel_id=1, source_target_pairs={{0,4},{4,0},{1,5},{5,1},{2,6},{6,2},{3,7},{7,3},{8,12},{12,8},{9,1... | collective-permute-start | bytes 884744 | tf_op jit(solution)/shard_map/ppermute | solution.py:30
  26.1 30.0 %copy-start.6 = (bf16[128,1152]{1,0:T(8,128)(2,1)}, bf16[128,1152]{1,0:T(8,128)(2,1)S(1)}, u32[]{:S(2)}) copy-start(bf16[128,1152]{1,0:T(8,128)(2,1)S(1)} %collective-permute-done.19) | copy-start | bytes 884740
  26.1 17.1 %collective-permute-start.13 = (bf16[128,1152]{1,0:T(8,128)(2,1)S(1)}, bf16[128,1152]{1,0:T(8,128)(2,1)S(1)}, u32[]{:S(2)}, u32[]{:S(2)}) collective-permute-start(bf16[128,1152]{1,0:T(8,128)(2,1)S(1)} %collective-permute-done.7), channel_id=1, source_target_pairs={{0,4},{4,0},{1,5},{5,1},{2,6},{6,2},{3,7},{7,3},{8,12},{12,8},{9,1... | collective-permute-start | bytes 884744 | tf_op jit(solution)/shard_map/ppermute | solution.py:30
  26.6 29.5 %copy-start.10 = (bf16[128,1152]{1,0:T(8,128)(2,1)}, bf16[128,1152]{1,0:T(8,128)(2,1)S(1)}, u32[]{:S(2)}) copy-start(bf16[128,1152]{1,0:T(8,128)(2,1)S(1)} %collective-permute-done.17) | copy-start | bytes 884740
  26.6 18.5 %collective-permute-start.18 = (bf16[128,1152]{1,0:T(8,128)(2,1)S(1)}, bf16[128,1152]{1,0:T(8,128)(2,1)}, u32[]{:S(2)}, u32[]{:S(2)}) collective-permute-start(bf16[128,1152]{1,0:T(8,128)(2,1)S(1)} %collective-permute-done.17), channel_id=1, source_target_pairs={{0,56},{8,0},{16,8},{24,16},{32,24},{40,32},{48,40},{56,48},{1,57}... | collective-permute-start | bytes 884744 | tf_op jit(solution)/shard_map/ppermute | solution.py:30
  29.8 26.3 %copy-start.11 = (bf16[128,1152]{1,0:T(8,128)(2,1)}, bf16[128,1152]{1,0:T(8,128)(2,1)S(1)}, u32[]{:S(2)}) copy-start(bf16[128,1152]{1,0:T(8,128)(2,1)S(1)} %collective-permute-done.11) | copy-start | bytes 884740
  29.8 10.1 %collective-permute-start.12 = (bf16[128,1152]{1,0:T(8,128)(2,1)S(1)}, bf16[128,1152]{1,0:T(8,128)(2,1)S(1)}, u32[]{:S(2)}, u32[]{:S(2)}) collective-permute-start(bf16[128,1152]{1,0:T(8,128)(2,1)S(1)} %collective-permute-done.11), channel_id=1, source_target_pairs={{0,56},{8,0},{16,8},{24,16},{32,24},{40,32},{48,40},{56,48},{1,57}... | collective-permute-start | bytes 884744 | tf_op jit(solution)/shard_map/ppermute | solution.py:30
  32.3 10.9 %collective-permute-start.9 = (bf16[128,1152]{1,0:T(8,128)(2,1)S(1)}, bf16[128,1152]{1,0:T(8,128)(2,1)S(1)}, u32[]{:S(2)}, u32[]{:S(2)}) collective-permute-start(bf16[128,1152]{1,0:T(8,128)(2,1)S(1)} %collective-permute-done.8), channel_id=1, source_target_pairs={{0,8},{8,16},{16,24},{24,32},{32,40},{40,48},{48,56},{56,0},{1,9},... | collective-permute-start | bytes 884744 | tf_op jit(solution)/shard_map/ppermute | solution.py:30
  39.9 16.3 %collective-permute-start.14 = (bf16[128,1152]{1,0:T(8,128)(2,1)S(1)}, bf16[128,1152]{1,0:T(8,128)(2,1)S(1)}, u32[]{:S(2)}, u32[]{:S(2)}) collective-permute-start(bf16[128,1152]{1,0:T(8,128)(2,1)S(1)} %collective-permute-done.12), channel_id=1, source_target_pairs={{0,56},{8,0},{16,8},{24,16},{32,24},{40,32},{48,40},{56,48},{1,57}... | collective-permute-start | bytes 884744 | tf_op jit(solution)/shard_map/ppermute | solution.py:30
  43.2 13.0 %collective-permute-start.15 = (bf16[128,1152]{1,0:T(8,128)(2,1)S(1)}, bf16[128,1152]{1,0:T(8,128)(2,1)S(1)}, u32[]{:S(2)}, u32[]{:S(2)}) collective-permute-start(bf16[128,1152]{1,0:T(8,128)(2,1)S(1)} %collective-permute-done.13), channel_id=1, source_target_pairs={{0,8},{8,16},{16,24},{24,32},{32,40},{40,48},{48,56},{56,0},{1,9},... | collective-permute-start | bytes 884744 | tf_op jit(solution)/shard_map/ppermute | solution.py:30
  43.2 13.0 %collective-permute-start.16 = (bf16[128,1152]{1,0:T(8,128)(2,1)S(1)}, bf16[128,1152]{1,0:T(8,128)(2,1)S(1)}, u32[]{:S(2)}, u32[]{:S(2)}) collective-permute-start(bf16[128,1152]{1,0:T(8,128)(2,1)S(1)} %collective-permute-done.9), channel_id=1, source_target_pairs={{0,4},{4,0},{1,5},{5,1},{2,6},{6,2},{3,7},{7,3},{8,12},{12,8},{9,1... | collective-permute-start | bytes 884744 | tf_op jit(solution)/shard_map/ppermute | solution.py:30
  64.6 14.0 %collective-permute-start.21 = (f16[52,32,128]{2,1,0:T(8,128)(2,1)}, f16[52,32,128]{2,1,0:T(8,128)(2,1)}, u32[]{:S(2)}, u32[]{:S(2)}) collective-permute-start(f16[52,32,128]{2,1,0:T(8,128)(2,1)} %get-tuple-element.86), channel_id=1, source_target_pairs={{0,1},{1,2},{2,3},{3,0},{4,5},{5,6},{6,7},{7,4},{8,9},{9,10},{10,1... | collective-permute-start | bytes 1277960 | tf_op jit(solution)/shard_map/ppermute | solution.py:30
  66.1 12.5 %collective-permute-start.23 = (f16[52,32,128]{2,1,0:T(8,128)(2,1)}, f16[52,32,128]{2,1,0:T(8,128)(2,1)}, u32[]{:S(2)}, u32[]{:S(2)}) collective-permute-start(f16[52,32,128]{2,1,0:T(8,128)(2,1)} %get-tuple-element.87), channel_id=1, source_target_pairs={{0,3},{1,0},{2,1},{3,2},{4,7},{5,4},{6,5},{7,6},{8,11},{9,8},{10,9... | collective-permute-start | bytes 1277960 | tf_op jit(solution)/shard_map/ppermute | solution.py:30
  68.9 14.8 %collective-permute-start.22 = (f16[52,32,128]{2,1,0:T(8,128)(2,1)}, f16[52,32,128]{2,1,0:T(8,128)(2,1)}, u32[]{:S(2)}, u32[]{:S(2)}) collective-permute-start(f16[52,32,128]{2,1,0:T(8,128)(2,1)} %get-tuple-element.88), channel_id=1, source_target_pairs={{0,2},{1,3},{2,0},{3,1},{4,6},{5,7},{6,4},{7,5},{8,10},{9,11},{10,... | collective-permute-start | bytes 1277960 | tf_op jit(solution)/shard_map/ppermute | solution.py:30
  70.7 30.9 %copy-start.2 = (bf16[112,32,128]{2,1,0:T(8,128)(2,1)S(1)}, bf16[112,32,128]{2,1,0:T(8,128)(2,1)}, u32[]{:S(2)}) copy-start(bf16[112,32,128]{2,1,0:T(8,128)(2,1)} %get-tuple-element.89.refs_4_) | copy-start | bytes 2752516
  85.4 16.1 %collective-permute-start.26 = (bf16[52,32,128]{2,1,0:T(8,128)(2,1)S(1)}, bf16[52,32,128]{2,1,0:T(8,128)(2,1)S(1)}, u32[]{:S(2)}, u32[]{:S(2)}) collective-permute-start(bf16[52,32,128]{2,1,0:T(8,128)(2,1)S(1)} %fusion.33.refs_0_), channel_id=1, source_target_pairs={{0,1},{1,2},{2,3},{3,0},{4,5},{5,6},{6,7},{7,4},{8,9},{9,10},{10,1... | collective-permute-start | bytes 1277960 | tf_op jit(solution)/shard_map/ppermute | solution.py:30
  86.2 15.2 %collective-permute-start.25 = (bf16[52,32,128]{2,1,0:T(8,128)(2,1)S(1)}, bf16[52,32,128]{2,1,0:T(8,128)(2,1)S(1)}, u32[]{:S(2)}, u32[]{:S(2)}) collective-permute-start(bf16[52,32,128]{2,1,0:T(8,128)(2,1)S(1)} %fusion.33.refs_0_), channel_id=1, source_target_pairs={{0,2},{1,3},{2,0},{3,1},{4,6},{5,7},{6,4},{7,5},{8,10},{9,11},{10,... | collective-permute-start | bytes 1277960 | tf_op jit(solution)/shard_map/ppermute | solution.py:30
  88.4 13.2 %collective-permute-start.24 = (bf16[52,32,128]{2,1,0:T(8,128)(2,1)S(1)}, bf16[52,32,128]{2,1,0:T(8,128)(2,1)S(1)}, u32[]{:S(2)}, u32[]{:S(2)}) collective-permute-start(bf16[52,32,128]{2,1,0:T(8,128)(2,1)S(1)} %fusion.33.refs_0_), channel_id=1, source_target_pairs={{0,3},{1,0},{2,1},{3,2},{4,7},{5,4},{6,5},{7,6},{8,11},{9,8},{10,9... | collective-permute-start | bytes 1277960 | tf_op jit(solution)/shard_map/ppermute | solution.py:30
  109.7 5.7 %collective-permute-start.27 = (bf16[1024,1152]{1,0:T(8,128)(2,1)S(1)}, bf16[1024,1152]{1,0:T(8,128)(2,1)S(1)}, u32[]{:S(2)}, u32[]{:S(2)}) collective-permute-start(bf16[1024,1152]{1,0:T(8,128)(2,1)S(1)} %fusion.18), channel_id=1, source_target_pairs={{0,64},{64,0},{1,65},{65,1},{2,66},{66,2},{3,67},{67,3},{4,68},{68... | collective-permute-start | bytes 7077896 | tf_op jit(solution)/shard_map/ppermute | solution.py:30
  115.8 15.8 %collective-permute-start.30 = (bf16[8,32,1152]{2,1,0:T(8,128)(2,1)S(1)}, bf16[8,32,1152]{2,1,0:T(8,128)(2,1)S(1)}, u32[]{:S(2)}, u32[]{:S(2)}) collective-permute-start(bf16[8,32,1152]{2,1,0:T(8,128)(2,1)S(1)} %bitcast.56), channel_id=1, source_target_pairs={{0,132},{4,0},{128,4},{132,128},{1,133},{5,1},{129,5},{133,129},{2... | collective-permute-start | bytes 1769480 | tf_op jit(solution)/shard_map/ppermute | solution.py:30
  117.6 27.4 %collective-permute-start.28 = (bf16[8,32,1152]{2,1,0:T(8,128)(2,1)S(1)}, bf16[8,32,1152]{2,1,0:T(8,128)(2,1)S(1)}, u32[]{:S(2)}, u32[]{:S(2)}) collective-permute-start(bf16[8,32,1152]{2,1,0:T(8,128)(2,1)S(1)} %bitcast.55), channel_id=1, source_target_pairs={{0,128},{4,132},{128,0},{132,4},{1,129},{5,133},{129,1},{133,5},{2... | collective-permute-start | bytes 1769480 | tf_op jit(solution)/shard_map/ppermute | solution.py:30
  118.7 27.4 %collective-permute-start.29 = (bf16[8,32,1152]{2,1,0:T(8,128)(2,1)S(1)}, bf16[8,32,1152]{2,1,0:T(8,128)(2,1)S(1)}, u32[]{:S(2)}, u32[]{:S(2)}) collective-permute-start(bf16[8,32,1152]{2,1,0:T(8,128)(2,1)S(1)} %bitcast.54), channel_id=1, source_target_pairs={{0,4},{4,128},{128,132},{132,0},{1,5},{5,129},{129,133},{133,1},{2... | collective-permute-start | bytes 1769480 | tf_op jit(solution)/shard_map/ppermute | solution.py:30
  (9 other events, 131.3 us)

commit v2 on v1

--- a/solution.py
+++ b/solution.py
@@ -22,7 +22,7 @@
 F32 = jnp.float32
 BF16 = jnp.bfloat16
 Y = ("yh", "yl")
-Y_WAYS = (2, 1, 3)
+Y_WAYS = (2, 1, 3, 0)
 
 
 def shift(axis, step, size):
@@ -36,15 +36,17 @@
 )
 
 
-def gather_tokens(rows):
+def gather_tokens(rows, early_work):
     up, down, swap = shift("z", 1, 8), shift("z", -1, 8), shift("yl", 1, 2)
     own, other = {0: rows}, {}
     own[-1], own[1], other[0] = up(own[0]), down(own[0]), swap(own[0])
     own[-2], own[2], other[-1] = up(own[-1]), down(own[1]), swap(own[-1])
     own[-3], own[3], other[1] = up(own[-2]), down(own[2]), swap(own[1])
     own[4], other[2], other[-2] = up(own[-3]), down(other[1]), swap(own[-2])
+    early = early_work([(own, other)[column][distance] for column, distance in ARRIVALS[:EARLY]])
+    early, own[4], other[2], other[-2] = lax.optimization_barrier((early, own[4], other[2], other[-2]))
     other[-3], other[3], other[4] = up(other[-2]), down(other[2]), swap(own[4])
-    return [(own, other)[column][distance] for column, distance in ARRIVALS]
+    return [(own, other)[column][distance] for column, distance in ARRIVALS], early
 
 
 def make_table(lists, places):
@@ -66,7 +68,9 @@
     starts = ends - counts
     rank = jnp.where(named, before.astype(jnp.int32) + starts[:, None], -1)
     far = ((tile >> 4) & 1) ^ places["core"]
-    target = (1 - far) * 32 + ((((tile >> 5) * 2 + (tile & 1)) - y) & 3) * 8 + ((tile >> 1) & 7)
+    along_y = (((tile >> 5) * 2 + (tile & 1)) - y) & 3
+    stand = sum(jnp.where(along_y == r, i, 0) for i, r in enumerate(Y_WAYS))
+    target = (1 - far) * 32 + stand * 8 + ((tile >> 1) & 7)
     code = (source + 1024 * target)[None, :] + 64 * block[:, None]
     slot = jnp.arange(SLOTS, dtype=jnp.int32)
     hit = rank.reshape(1, -1) == slot[:, None]
@@ -197,12 +201,25 @@
     return jnp.zeros((SLOTS - FAST, TILE, BLOCK), BF16)
 
 
-def reduce_tokens(mine, other):
-    mine = mine.reshape(4, 8, TILE, WIDTH)
-    other = other.reshape(4, 8, TILE, WIDTH)
-    got = [shift(Y, r, 4)((mine[r] + other[r].astype(F32)).astype(BF16)) for r in Y_WAYS]
-    column = mine[0] + other[0].astype(F32) + got[0].astype(F32) + got[1].astype(F32) + got[2].astype(F32)
-    got = lax.all_to_all(column.astype(BF16), "z", 0, 0, tiled=True)
+def reduce_tokens(acts, w_dec):
+    half, group = TILES * TILE // 2, 8 * TILE
+    chunks = []
+    for start, stop in ((0, group), (group, half)):
+        theirs = jnp.dot(acts[start:stop], w_dec, preferred_element_type=F32).astype(BF16)
+        other = shift("core", 1, 2)(theirs)
+        if chunks:
+            acts, theirs, chunks[0] = lax.optimization_barrier((acts, theirs, chunks[0]))
+        else:
+            acts, theirs = lax.optimization_barrier((acts, theirs))
+        mine = jnp.dot(acts[half + start : half + stop], w_dec, preferred_element_type=F32)
+        acts, mine = lax.optimization_barrier((acts, mine))
+        whole = mine + other.astype(F32)
+        if not chunks:
+            whole = whole.astype(BF16)
+        chunks += [whole[i : i + group] for i in range(0, stop - start, group)]
+    got = [shift(Y, r, 4)(c.astype(BF16)) for r, c in zip(Y_WAYS[:3], chunks)]
+    column = chunks[3] + got[0].astype(F32) + got[1].astype(F32) + got[2].astype(F32)
+    got = lax.all_to_all(column.astype(BF16).reshape(8, TILE, WIDTH), "z", 0, 0, tiled=True)
     return jnp.sum(got.astype(F32), axis=0).astype(BF16)
 
 
@@ -211,21 +228,14 @@
     w_enc, w_dec = w_enc[0], w_dec[0]
     thresholds = threshold_level[0].reshape(BPO, BLOCK)
     table, facts = make_table(block_lists[0], places)
-    gathered = gather_tokens(resid[0])
-    if EARLY:
-        pre = encode(0, (0, 1), 0, FAST, table, facts, gathered[:EARLY], w_enc)
-        pre = encode(EARLY, (1, 2), 0, FAST, table, facts, gathered[EARLY:], w_enc, pre)
-    else:
-        pre = encode(0, (0, 2), 0, FAST, table, facts, gathered, w_enc)
+    gathered, early = gather_tokens(
+        resid[0], lambda arrived: encode(0, (0, 1), 0, FAST, table, facts, arrived, w_enc)
+    )
+    pre = encode(EARLY, (1, 2), 0, FAST, table, facts, gathered[EARLY:], w_enc, early)
     pieces = activate(0, FAST, pre, table, thresholds, places)
     more = lax.cond(facts[3 * BPO] > FAST, some_more, no_more, table, facts, thresholds, w_enc, places, *gathered)
     acts = place(table, facts, pieces + (more,))
-    half = TILES * TILE // 2
-    theirs = jnp.dot(acts[:half], w_dec, preferred_element_type=F32).astype(BF16)
-    other = shift("core", 1, 2)(theirs)
-    acts, theirs = lax.optimization_barrier((acts, theirs))
-    mine = jnp.dot(acts[half:], w_dec, preferred_element_type=F32)
-    return reduce_tokens(mine, other)
+    return reduce_tokens(acts, w_dec)
 
 
 def solution(mesh):

time: 173 us -> 169 us (0.977)
  waiting for transfers between devices: 70.9 us -> 64.8 us
  starting transfers between devices: 34.7 us -> 37.3 us
    ppermute x25 -> x26, waiting for transfers between devices: 70.9 us -> 64.8 us  [shift(): return lambda value: lax.ppermute(value, axis, pairs)]
    ppermute x25 -> x26, starting transfers between devices: 34.7 us -> 37.3 us  [shift(): return lambda value: lax.ppermute(value, axis, pairs)]
    dot_general x2 -> x4, matrix products: 11.3 us -> 11.5 us  [the longest x2 5.76 us: reduce_tokens(): jnp.dot(acts[start:stop], w_dec, preferred_element_type=F32).astype(BF16)]
  transfers between devices with their start and end apart: 25 -> 26, of which waited for: 11 -> 12; matrix products, arithmetic and copies ran while one was open for 6% -> 9% of each run, Pallas kernels for 6% -> 6%
where the time goes in v2:
time: 169 us; the launch traced here: 168 us
  waiting for transfers between devices  64.8 us (38%)
  starting transfers between devices  37.3 us (22%)
  blocking collectives  24.2 us (14%)
  Pallas kernels  20.5 us (12%)
  matrix products  11.9 us (7%)
  other arithmetic  5.95 us (4%)
  local copies, waits for them, and re-layouts  2.65 us (2%)
    ppermute x26, waiting for transfers between devices, shift(): return lambda value: lax.ppermute(value, axis, pairs)  64.8 us
    ppermute x26, starting transfers between devices, shift(): return lambda value: lax.ppermute(value, axis, pairs)  37.3 us
    all_to_all x1, blocking collectives, reduce_tokens(): lax.all_to_all(column.astype(BF16).reshape(8, TILE, WIDTH), 'z', 0, 0, ti...  24.2 us
    pallas_call x2, Pallas kernels, encode(): pl.pallas_call(functools.partial(encode_kernel, count, lead, bounds, low,...  17.1 us
    dot_general x2, matrix products, reduce_tokens(): jnp.dot(acts[start:stop], w_dec, preferred_element_type=F32).astype(BF16)  5.76 us
    dot_general x2, matrix products, reduce_tokens(): jnp.dot(acts[half + start:half + stop], w_dec, preferred_element_type=F32)  5.75 us
    pallas_call x1, Pallas kernels, place(): pl.pallas_call(place_kernel, out_shape=jax.ShapeDtypeStruct((TILES * TILE...  3.4 us
  transfers between devices with their start and end apart: 26, of which 12 were waited for; matrix products, arithmetic and copies ran while one was open for 9% of the time, Pallas kernels for 6%

profile of v2, /device:TPU:8, one launch (start us, length us, event | category | flops | bytes accessed | tf_op | source)
XLA Modules:
  0.0 168.2 jit_solution(4803226987607755839)
XLA Ops:
  0.0 2.2 %collective-permute-start.12 = (bf16[128,1152]{1,0:T(8,128)(2,1)}, bf16[128,1152]{1,0:T(8,128)(2,1)S(1)}, u32[]{:S(2)}, u32[]{:S(2)}) collective-permute-start(bf16[128,1152]{1,0:T(8,128)(2,1)} %bitcast.72), channel_id=1, source_target_pairs={{0,4},{4,0},{1,5},{5,1},{2,6},{6,2},{3,7},{7,3},{8,12},{12,8},{9,1... | collective-permute-start | bytes 884744 | tf_op jit(solution)/shard_map/ppermute | solution.py:30
  2.4 3.9 %collective-permute-start.6 = (bf16[128,1152]{1,0:T(8,128)(2,1)}, bf16[128,1152]{1,0:T(8,128)(2,1)S(1)}, u32[]{:S(2)}, u32[]{:S(2)}) collective-permute-start(bf16[128,1152]{1,0:T(8,128)(2,1)} %bitcast.74), channel_id=1, source_target_pairs={{0,56},{8,0},{16,8},{24,16},{32,24},{40,32},{48,40},{56,48},{1,57}... | collective-permute-start | bytes 884744 | tf_op jit(solution)/shard_map/ppermute | solution.py:30
  7.7 5.5 %collective-permute-done.7 = bf16[128,1152]{1,0:T(8,128)(2,1)S(1)} collective-permute-done((bf16[128,1152]{1,0:T(8,128)(2,1)}, bf16[128,1152]{1,0:T(8,128)(2,1)S(1)}, u32[]{:S(2)}, u32[]{:S(2)}) %collective-permute-start.7) | collective-permute-done | bytes 294944 | tf_op jit(solution)/shard_map/ppermute | solution.py:30
  13.3 3.2 %collective-permute-start.8 = (bf16[128,1152]{1,0:T(8,128)(2,1)S(1)}, bf16[128,1152]{1,0:T(8,128)(2,1)S(1)}, u32[]{:S(2)}, u32[]{:S(2)}) collective-permute-start(bf16[128,1152]{1,0:T(8,128)(2,1)S(1)} %collective-permute-done.6), channel_id=1, source_target_pairs={{0,56},{8,0},{16,8},{24,16},{32,24},{40,32},{48,40},{56,48},{1,57}... | collective-permute-start | bytes 884744 | tf_op jit(solution)/shard_map/ppermute | solution.py:30
  16.7 1.6 collective-permute-start.13
  18.7 3.7 %collective-permute-done.9 = bf16[128,1152]{1,0:T(8,128)(2,1)S(1)} collective-permute-done((bf16[128,1152]{1,0:T(8,128)(2,1)S(1)}, bf16[128,1152]{1,0:T(8,128)(2,1)S(1)}, u32[]{:S(2)}, u32[]{:S(2)}) %collective-permute-start.9) | collective-permute-done | bytes 294944 | tf_op jit(solution)/shard_map/ppermute | solution.py:30
  22.4 3.2 %collective-permute-start.10 = (bf16[128,1152]{1,0:T(8,128)(2,1)S(1)}, bf16[128,1152]{1,0:T(8,128)(2,1)S(1)}, u32[]{:S(2)}, u32[]{:S(2)}) collective-permute-start(bf16[128,1152]{1,0:T(8,128)(2,1)S(1)} %collective-permute-done.8), channel_id=1, source_target_pairs={{0,56},{8,0},{16,8},{24,16},{32,24},{40,32},{48,40},{56,48},{1,57}... | collective-permute-start | bytes 884744 | tf_op jit(solution)/shard_map/ppermute | solution.py:30
  27.2 1.7 collective-permute-start.17
  28.8 4.1 %collective-permute-done.14 = bf16[128,1152]{1,0:T(8,128)(2,1)S(1)} collective-permute-done((bf16[128,1152]{1,0:T(8,128)(2,1)S(1)}, bf16[128,1152]{1,0:T(8,128)(2,1)S(1)}, u32[]{:S(2)}, u32[]{:S(2)}) %collective-permute-start.14) | collective-permute-done | bytes 294944 | tf_op jit(solution)/shard_map/ppermute | solution.py:30
  35.0 10.8 %encode.4.refs_7_ = f32[208,32,128]{2,1,0:T(8,128)S(1)} custom-call(s32[320]{0:T(512)S(1)} %multiply_add_fusion.table, s32[50]{0:T(128)S(1)} %concatenate.6.facts, bf16[4,32,1152]{2,1,0:T(8,128)(2,1)} %bitcast.75, bf16[4,32,1152]{2,1,0:T(8,128)(2,1)S(1)} %bitcast.81, bf16[4,32,1152]{2,1,0:T(8,128)(2,1)S(1)} %bitcast.79, bf16[4,32,1152]{2,1,0:T(8,128)(2,1)S(1)} %bitcast.85, ...), custom_call_target="tpu_custom_call" | custom-call | flops 5000000000 | bytes 4000000 | tf_op jit(solution)/shard_map/encode/pallas_call | solution.py:122
  47.3 2.1 %collective-permute-start.18 = (bf16[128,1152]{1,0:T(8,128)(2,1)S(1)}, bf16[128,1152]{1,0:T(8,128)(2,1)S(1)}, u32[]{:S(2)}, u32[]{:S(2)}) collective-permute-start(bf16[128,1152]{1,0:T(8,128)(2,1)S(1)} %collective-permute-done.16), channel_id=1, source_target_pairs={{0,56},{8,0},{16,8},{24,16},{32,24},{40,32},{48,40},{56,48},{1,57}... | collective-permute-start | bytes 884744 | tf_op jit(solution)/shard_map/ppermute | solution.py:30
  50.0 2.8 %collective-permute-done.20 = bf16[128,1152]{1,0:T(8,128)(2,1)S(1)} collective-permute-done((bf16[128,1152]{1,0:T(8,128)(2,1)S(1)}, bf16[128,1152]{1,0:T(8,128)(2,1)S(1)}, u32[]{:S(2)}, u32[]{:S(2)}) %collective-permute-start.20) | collective-permute-done | bytes 294944 | tf_op jit(solution)/shard_map/ppermute | solution.py:30
  54.0 3.3 %collective-permute-done.19 = bf16[128,1152]{1,0:T(8,128)(2,1)S(1)} collective-permute-done((bf16[128,1152]{1,0:T(8,128)(2,1)S(1)}, bf16[128,1152]{1,0:T(8,128)(2,1)S(1)}, u32[]{:S(2)}, u32[]{:S(2)}) %collective-permute-start.19) | collective-permute-done | bytes 294944 | tf_op jit(solution)/shard_map/ppermute | solution.py:30
  57.3 6.3 %encode.5 = f32[208,32,128]{2,1,0:T(8,128)S(1)} custom-call(s32[320]{0:T(512)S(1)} %multiply_add_fusion.table, s32[50]{0:T(128)S(1)} %concatenate.6.facts, bf16[4,32,1152]{2,1,0:T(8,128)(2,1)S(1)} %bitcast.61, bf16[4,32,1152]{2,1,0:T(8,128)(2,1)S(1)} %bitcast.59, bf16[4,32,1152]{2,1,0:T(8,128)(2,1)S(1)} %bitcast.57, bf16[4,32,1152]{2,1,0:T(8,128)(2,1)S(1)} %bitcast.65, ...), custom_call_target="tpu_custom_call" | custom-call | flops 3000000000 | bytes 4000000 | tf_op jit(solution)/shard_map/encode/pallas_call | solution.py:122
  66.3 1.8 %collective-permute-start.23 = (f16[52,32,128]{2,1,0:T(8,128)(2,1)}, f16[52,32,128]{2,1,0:T(8,128)(2,1)}, u32[]{:S(2)}, u32[]{:S(2)}) collective-permute-start(f16[52,32,128]{2,1,0:T(8,128)(2,1)} %get-tuple-element.103), channel_id=1, source_target_pairs={{0,3},{1,0},{2,1},{3,2},{4,7},{5,4},{6,5},{7,6},{8,11},{9,8},{10,9... | collective-permute-start | bytes 1277960 | tf_op jit(solution)/shard_map/ppermute | solution.py:30
  69.1 1.8 %collective-permute-start.22 = (f16[52,32,128]{2,1,0:T(8,128)(2,1)}, f16[52,32,128]{2,1,0:T(8,128)(2,1)}, u32[]{:S(2)}, u32[]{:S(2)}) collective-permute-start(f16[52,32,128]{2,1,0:T(8,128)(2,1)} %get-tuple-element.104), channel_id=1, source_target_pairs={{0,2},{1,3},{2,0},{3,1},{4,6},{5,7},{6,4},{7,5},{8,10},{9,11},{10,... | collective-permute-start | bytes 1277960 | tf_op jit(solution)/shard_map/ppermute | solution.py:30
  71.2 5.1 %collective-permute-done.21 = f16[52,32,128]{2,1,0:T(8,128)(2,1)} collective-permute-done((f16[52,32,128]{2,1,0:T(8,128)(2,1)}, f16[52,32,128]{2,1,0:T(8,128)(2,1)}, u32[]{:S(2)}, u32[]{:S(2)}) %collective-permute-start.21) | collective-permute-done | bytes 426016 | tf_op jit(solution)/shard_map/ppermute | solution.py:30
  76.4 7.5 %collective-permute-done.22 = f16[52,32,128]{2,1,0:T(8,128)(2,1)} collective-permute-done((f16[52,32,128]{2,1,0:T(8,128)(2,1)}, f16[52,32,128]{2,1,0:T(8,128)(2,1)}, u32[]{:S(2)}, u32[]{:S(2)}) %collective-permute-start.22) | collective-permute-done | bytes 426016 | tf_op jit(solution)/shard_map/ppermute | solution.py:30
  83.9 1.7 %fusion.40.refs_0_ = bf16[52,32,128]{2,1,0:T(8,128)(2,1)S(1)} fusion(f32[208,32,128]{2,1,0:T(8,128)S(1)} %encode.5, f16[52,32,128]{2,1,0:T(8,128)(2,1)} %collective-permute-done.23, f16[52,32,128]{2,1,0:T(8,128)(2,1)} %collective-permute-done.22, f16[52,32,128]{2,1,0:T(8,128)(2,1)} %collective-permute-done.21, f32[52,128]{1,0:T(8,128)S(1)} %fusion.42), kind=kLoop, calls=%fused_computation.53 | loop fusion | flops 2129920 | bytes 2582528 | tf_op jit(solution)/shard_map/convert_element_type | solution.py:191
  86.6 4.3 %collective-permute-start.25 = (bf16[52,32,128]{2,1,0:T(8,128)(2,1)S(1)}, bf16[52,32,128]{2,1,0:T(8,128)(2,1)S(1)}, u32[]{:S(2)}, u32[]{:S(2)}) collective-permute-start(bf16[52,32,128]{2,1,0:T(8,128)(2,1)S(1)} %fusion.40.refs_0_), channel_id=1, source_target_pairs={{0,2},{1,3},{2,0},{3,1},{4,6},{5,7},{6,4},{7,5},{8,10},{9,11},{10,... | collective-permute-start | bytes 1277960 | tf_op jit(solution)/shard_map/ppermute | solution.py:30
  90.8 4.6 %collective-permute-done.26.refs_3_ = bf16[52,32,128]{2,1,0:T(8,128)(2,1)S(1)} collective-permute-done((bf16[52,32,128]{2,1,0:T(8,128)(2,1)S(1)}, bf16[52,32,128]{2,1,0:T(8,128)(2,1)S(1)}, u32[]{:S(2)}, u32[]{:S(2)}) %collective-permute-start.26) | collective-permute-done | bytes 426016 | tf_op jit(solution)/shard_map/ppermute | solution.py:30
  95.5 6.0 %collective-permute-done.25.refs_2_ = bf16[52,32,128]{2,1,0:T(8,128)(2,1)S(1)} collective-permute-done((bf16[52,32,128]{2,1,0:T(8,128)(2,1)S(1)}, bf16[52,32,128]{2,1,0:T(8,128)(2,1)S(1)}, u32[]{:S(2)}, u32[]{:S(2)}) %collective-permute-start.25) | collective-permute-done | bytes 426016 | tf_op jit(solution)/shard_map/ppermute | solution.py:30
  101.5 3.4 %place.1 = bf16[2048,2048]{1,0:T(8,128)(2,1)S(1)} custom-call(s32[320]{0:T(512)S(1)} %multiply_add_fusion.table, s32[50]{0:T(128)S(1)} %concatenate.6.facts, bf16[52,32,128]{2,1,0:T(8,128)(2,1)S(1)} %fusion.40.refs_0_, bf16[52,32,128]{2,1,0:T(8,128)(2,1)S(1)} %collective-permute-done.24.refs_1_, bf16[52,32,128]{2,1,0:T(8,128)(2,1)S(1)} %collective-permute-done.25.refs_2_, ...), custom_call_target="tpu_custom_call" | custom-call | flops 1000000 | bytes 8000000 | tf_op jit(solution)/shard_map/place/pallas_call | solution.py:169
  104.9 1.5 fusion.25
  106.6 1.5 fusion.16
  108.1 4.2 %fusion.20 = bf16[768,1152]{1,0:T(8,128)(2,1)S(1)} fusion(bf16[1,2048,1152]{2,1,0:T(8,128)(2,1)S(1)} %bitcast.71, bf16[2048,2048]{1,0:T(8,128)(2,1)S(1)} %place.1), kind=kOutput, calls=%fused_computation.28 | convolution fusion | flops 3624763392 | bytes 9633792 | tf_op jit(solution)/shard_map/dot_general | solution.py:208
  113.0 2.3 %collective-permute-start.29 = (bf16[256,1152]{1,0:T(8,128)(2,1)S(1)}, bf16[256,1152]{1,0:T(8,128)(2,1)S(1)}, u32[]{:S(2)}, u32[]{:S(2)}) collective-permute-start(bf16[256,1152]{1,0:T(8,128)(2,1)S(1)} %add_convert_fusion), channel_id=1, source_target_pairs={{0,128},{4,132},{128,0},{132,4},{1,129},{5,133},{129,1},{133,5},{2... | collective-permute-start | bytes 1769480 | tf_op jit(solution)/shard_map/ppermute | solution.py:30
  115.4 4.2 %fusion.12 = f32[768,1152]{1,0:T(8,128)S(1)} fusion(bf16[1,2048,1152]{2,1,0:T(8,128)(2,1)S(1)} %bitcast.71, bf16[2048,2048]{1,0:T(8,128)(2,1)S(1)} %place.1), kind=kOutput, calls=%fused_computation.19 | convolution fusion | flops 3623878656 | bytes 11403264 | tf_op jit(solution)/shard_map/dot_general | solution.py:214
  120.2 2.0 %collective-permute-start.31 = (bf16[256,1152]{1,0:T(8,128)(2,1)S(1)}, bf16[256,1152]{1,0:T(8,128)(2,1)S(1)}, u32[]{:S(2)}, u32[]{:S(2)}) collective-permute-start(bf16[256,1152]{1,0:T(8,128)(2,1)S(1)} %get-tuple-element.106), channel_id=1, source_target_pairs={{0,132},{4,0},{128,4},{132,128},{1,133},{5,1},{129,5},{133,129},{2... | collective-permute-start | bytes 1769480 | tf_op jit(solution)/shard_map/ppermute | solution.py:30
  122.2 8.6 %collective-permute-done.29 = bf16[256,1152]{1,0:T(8,128)(2,1)S(1)} collective-permute-done((bf16[256,1152]{1,0:T(8,128)(2,1)S(1)}, bf16[256,1152]{1,0:T(8,128)(2,1)S(1)}, u32[]{:S(2)}, u32[]{:S(2)}) %collective-permute-start.29) | collective-permute-done | bytes 589856 | tf_op jit(solution)/shard_map/ppermute | solution.py:30
  130.9 12.2 %collective-permute-done.30 = bf16[256,1152]{1,0:T(8,128)(2,1)S(1)} collective-permute-done((bf16[256,1152]{1,0:T(8,128)(2,1)S(1)}, bf16[256,1152]{1,0:T(8,128)(2,1)S(1)}, u32[]{:S(2)}, u32[]{:S(2)}) %collective-permute-start.30) | collective-permute-done | bytes 589856 | tf_op jit(solution)/shard_map/ppermute | solution.py:30
  143.3 24.2 %all_to_all.5 = bf16[8,32,1152]{2,1,0:T(8,128)(2,1)S(1)} all-to-all(bf16[8,32,1152]{2,1,0:T(8,128)(2,1)S(1)} %bitcast.56), channel_id=1, replica_groups=mesh['yh'=2,'core'=2,'z'=8,'yl'=2,'x'=4] {'z'}, dimensions={0} | all-to-all | bytes 1179648 | tf_op jit(solution)/shard_map/all_to_all | solution.py:222
  (82 shorter events, 16.8 us)
Async XLA Ops:
  0.0 27.2 %collective-permute-start.12 = (bf16[128,1152]{1,0:T(8,128)(2,1)}, bf16[128,1152]{1,0:T(8,128)(2,1)S(1)}, u32[]{:S(2)}, u32[]{:S(2)}) collective-permute-start(bf16[128,1152]{1,0:T(8,128)(2,1)} %bitcast.72), channel_id=1, source_target_pairs={{0,4},{4,0},{1,5},{5,1},{2,6},{6,2},{3,7},{7,3},{8,12},{12,8},{9,1... | collective-permute-start | bytes 884744 | tf_op jit(solution)/shard_map/ppermute | solution.py:30
  2.2 11.1 %collective-permute-start.7 = (bf16[128,1152]{1,0:T(8,128)(2,1)}, bf16[128,1152]{1,0:T(8,128)(2,1)S(1)}, u32[]{:S(2)}, u32[]{:S(2)}) collective-permute-start(bf16[128,1152]{1,0:T(8,128)(2,1)} %bitcast.73), channel_id=1, source_target_pairs={{0,8},{8,16},{16,24},{24,32},{32,40},{40,48},{48,56},{56,0},{1,9},... | collective-permute-start | bytes 884744 | tf_op jit(solution)/shard_map/ppermute | solution.py:30
  2.4 10.9 %collective-permute-start.6 = (bf16[128,1152]{1,0:T(8,128)(2,1)}, bf16[128,1152]{1,0:T(8,128)(2,1)S(1)}, u32[]{:S(2)}, u32[]{:S(2)}) collective-permute-start(bf16[128,1152]{1,0:T(8,128)(2,1)} %bitcast.74), channel_id=1, source_target_pairs={{0,56},{8,0},{16,8},{24,16},{32,24},{40,32},{48,40},{56,48},{1,57}... | collective-permute-start | bytes 884744 | tf_op jit(solution)/shard_map/ppermute | solution.py:30
  13.3 32.6 %copy-start.3 = (bf16[128,1152]{1,0:T(8,128)(2,1)}, bf16[128,1152]{1,0:T(8,128)(2,1)S(1)}, u32[]{:S(2)}) copy-start(bf16[128,1152]{1,0:T(8,128)(2,1)S(1)} %collective-permute-done.7) | copy-start | bytes 884740
  13.3 9.1 %collective-permute-start.9 = (bf16[128,1152]{1,0:T(8,128)(2,1)S(1)}, bf16[128,1152]{1,0:T(8,128)(2,1)S(1)}, u32[]{:S(2)}, u32[]{:S(2)}) collective-permute-start(bf16[128,1152]{1,0:T(8,128)(2,1)S(1)} %collective-permute-done.7), channel_id=1, source_target_pairs={{0,8},{8,16},{16,24},{24,32},{32,40},{40,48},{48,56},{56,0},{1,9},... | collective-permute-start | bytes 884744 | tf_op jit(solution)/shard_map/ppermute | solution.py:30
  13.3 32.6 %copy-start.4 = (bf16[128,1152]{1,0:T(8,128)(2,1)}, bf16[128,1152]{1,0:T(8,128)(2,1)S(1)}, u32[]{:S(2)}) copy-start(bf16[128,1152]{1,0:T(8,128)(2,1)S(1)} %collective-permute-done.6) | copy-start | bytes 884740
  13.3 9.1 %collective-permute-start.8 = (bf16[128,1152]{1,0:T(8,128)(2,1)S(1)}, bf16[128,1152]{1,0:T(8,128)(2,1)S(1)}, u32[]{:S(2)}, u32[]{:S(2)}) collective-permute-start(bf16[128,1152]{1,0:T(8,128)(2,1)S(1)} %collective-permute-done.6), channel_id=1, source_target_pairs={{0,56},{8,0},{16,8},{24,16},{32,24},{40,32},{48,40},{56,48},{1,57}... | collective-permute-start | bytes 884744 | tf_op jit(solution)/shard_map/ppermute | solution.py:30
  16.7 18.3 %collective-permute-start.13 = (bf16[128,1152]{1,0:T(8,128)(2,1)S(1)}, bf16[128,1152]{1,0:T(8,128)(2,1)S(1)}, u32[]{:S(2)}, u32[]{:S(2)}) collective-permute-start(bf16[128,1152]{1,0:T(8,128)(2,1)S(1)} %collective-permute-done.7), channel_id=1, source_target_pairs={{0,4},{4,0},{1,5},{5,1},{2,6},{6,2},{3,7},{7,3},{8,12},{12,8},{9,1... | collective-permute-start | bytes 884744 | tf_op jit(solution)/shard_map/ppermute | solution.py:30
  18.2 14.7 %collective-permute-start.14 = (bf16[128,1152]{1,0:T(8,128)(2,1)S(1)}, bf16[128,1152]{1,0:T(8,128)(2,1)S(1)}, u32[]{:S(2)}, u32[]{:S(2)}) collective-permute-start(bf16[128,1152]{1,0:T(8,128)(2,1)S(1)} %collective-permute-done.6), channel_id=1, source_target_pairs={{0,4},{4,0},{1,5},{5,1},{2,6},{6,2},{3,7},{7,3},{8,12},{12,8},{9,1... | collective-permute-start | bytes 884744 | tf_op jit(solution)/shard_map/ppermute | solution.py:30
  22.4 23.5 %copy-start.5 = (bf16[128,1152]{1,0:T(8,128)(2,1)}, bf16[128,1152]{1,0:T(8,128)(2,1)S(1)}, u32[]{:S(2)}) copy-start(bf16[128,1152]{1,0:T(8,128)(2,1)S(1)} %collective-permute-done.9) | copy-start | bytes 884740
  22.4 11.1 %collective-permute-start.11 = (bf16[128,1152]{1,0:T(8,128)(2,1)S(1)}, bf16[128,1152]{1,0:T(8,128)(2,1)S(1)}, u32[]{:S(2)}, u32[]{:S(2)}) collective-permute-start(bf16[128,1152]{1,0:T(8,128)(2,1)S(1)} %collective-permute-done.9), channel_id=1, source_target_pairs={{0,8},{8,16},{16,24},{24,32},{32,40},{40,48},{48,56},{56,0},{1,9},... | collective-permute-start | bytes 884744 | tf_op jit(solution)/shard_map/ppermute | solution.py:30
  22.4 23.5 %copy-start.6 = (bf16[128,1152]{1,0:T(8,128)(2,1)}, bf16[128,1152]{1,0:T(8,128)(2,1)S(1)}, u32[]{:S(2)}) copy-start(bf16[128,1152]{1,0:T(8,128)(2,1)S(1)} %collective-permute-done.8) | copy-start | bytes 884740
  22.4 12.6 %collective-permute-start.10 = (bf16[128,1152]{1,0:T(8,128)(2,1)S(1)}, bf16[128,1152]{1,0:T(8,128)(2,1)S(1)}, u32[]{:S(2)}, u32[]{:S(2)}) collective-permute-start(bf16[128,1152]{1,0:T(8,128)(2,1)S(1)} %collective-permute-done.8), channel_id=1, source_target_pairs={{0,56},{8,0},{16,8},{24,16},{32,24},{40,32},{48,40},{56,48},{1,57}... | collective-permute-start | bytes 884744 | tf_op jit(solution)/shard_map/ppermute | solution.py:30
  27.2 18.8 %collective-permute-start.17 = (bf16[128,1152]{1,0:T(8,128)(2,1)S(1)}, bf16[128,1152]{1,0:T(8,128)(2,1)S(1)}, u32[]{:S(2)}, u32[]{:S(2)}) collective-permute-start(bf16[128,1152]{1,0:T(8,128)(2,1)S(1)} %collective-permute-done.9), channel_id=1, source_target_pairs={{0,4},{4,0},{1,5},{5,1},{2,6},{6,2},{3,7},{7,3},{8,12},{12,8},{9,1... | collective-permute-start | bytes 884744 | tf_op jit(solution)/shard_map/ppermute | solution.py:30
  32.9 13.0 %collective-permute-start.16 = (bf16[128,1152]{1,0:T(8,128)(2,1)S(1)}, bf16[128,1152]{1,0:T(8,128)(2,1)S(1)}, u32[]{:S(2)}, u32[]{:S(2)}) collective-permute-start(bf16[128,1152]{1,0:T(8,128)(2,1)S(1)} %collective-permute-done.14), channel_id=1, source_target_pairs={{0,56},{8,0},{16,8},{24,16},{32,24},{40,32},{48,40},{56,48},{1,57}... | collective-permute-start | bytes 884744 | tf_op jit(solution)/shard_map/ppermute | solution.py:30
  33.4 12.5 %collective-permute-start.15 = (bf16[128,1152]{1,0:T(8,128)(2,1)S(1)}, bf16[128,1152]{1,0:T(8,128)(2,1)S(1)}, u32[]{:S(2)}, u32[]{:S(2)}) collective-permute-start(bf16[128,1152]{1,0:T(8,128)(2,1)S(1)} %collective-permute-done.11), channel_id=1, source_target_pairs={{0,8},{8,16},{16,24},{24,32},{32,40},{40,48},{48,56},{56,0},{1,9},... | collective-permute-start | bytes 884744 | tf_op jit(solution)/shard_map/ppermute | solution.py:30
  35.0 22.3 %copy-start.1 = (bf16[1,1152,2048]{2,1,0:T(8,128)(2,1)S(1)}, bf16[1,1152,2048]{2,1,0:T(8,128)(2,1)}, u32[]{:S(2)}) copy-start(bf16[1,1152,2048]{2,1,0:T(8,128)(2,1)} %param.10) | copy-start | bytes 14155780
  46.0 6.8 %collective-permute-start.20 = (bf16[128,1152]{1,0:T(8,128)(2,1)S(1)}, bf16[128,1152]{1,0:T(8,128)(2,1)S(1)}, u32[]{:S(2)}, u32[]{:S(2)}) collective-permute-start(bf16[128,1152]{1,0:T(8,128)(2,1)S(1)} %collective-permute-done.15), channel_id=1, source_target_pairs={{0,4},{4,0},{1,5},{5,1},{2,6},{6,2},{3,7},{7,3},{8,12},{12,8},{9,1... | collective-permute-start | bytes 884744 | tf_op jit(solution)/shard_map/ppermute | solution.py:30
  47.3 6.7 %collective-permute-start.18 = (bf16[128,1152]{1,0:T(8,128)(2,1)S(1)}, bf16[128,1152]{1,0:T(8,128)(2,1)S(1)}, u32[]{:S(2)}, u32[]{:S(2)}) collective-permute-start(bf16[128,1152]{1,0:T(8,128)(2,1)S(1)} %collective-permute-done.16), channel_id=1, source_target_pairs={{0,56},{8,0},{16,8},{24,16},{32,24},{40,32},{48,40},{56,48},{1,57}... | collective-permute-start | bytes 884744 | tf_op jit(solution)/shard_map/ppermute | solution.py:30
  49.4 7.9 %collective-permute-start.19 = (bf16[128,1152]{1,0:T(8,128)(2,1)S(1)}, bf16[128,1152]{1,0:T(8,128)(2,1)S(1)}, u32[]{:S(2)}, u32[]{:S(2)}) collective-permute-start(bf16[128,1152]{1,0:T(8,128)(2,1)S(1)} %collective-permute-done.17), channel_id=1, source_target_pairs={{0,8},{8,16},{16,24},{24,32},{32,40},{40,48},{48,56},{56,0},{1,9},... | collective-permute-start | bytes 884744 | tf_op jit(solution)/shard_map/ppermute | solution.py:30
  64.8 11.5 %collective-permute-start.21 = (f16[52,32,128]{2,1,0:T(8,128)(2,1)}, f16[52,32,128]{2,1,0:T(8,128)(2,1)}, u32[]{:S(2)}, u32[]{:S(2)}) collective-permute-start(f16[52,32,128]{2,1,0:T(8,128)(2,1)} %get-tuple-element.102), channel_id=1, source_target_pairs={{0,1},{1,2},{2,3},{3,0},{4,5},{5,6},{6,7},{7,4},{8,9},{9,10},{10,1... | collective-permute-start | bytes 1277960 | tf_op jit(solution)/shard_map/ppermute | solution.py:30
  66.3 10.1 %collective-permute-start.23 = (f16[52,32,128]{2,1,0:T(8,128)(2,1)}, f16[52,32,128]{2,1,0:T(8,128)(2,1)}, u32[]{:S(2)}, u32[]{:S(2)}) collective-permute-start(f16[52,32,128]{2,1,0:T(8,128)(2,1)} %get-tuple-element.103), channel_id=1, source_target_pairs={{0,3},{1,0},{2,1},{3,2},{4,7},{5,4},{6,5},{7,6},{8,11},{9,8},{10,9... | collective-permute-start | bytes 1277960 | tf_op jit(solution)/shard_map/ppermute | solution.py:30
  69.1 14.7 %collective-permute-start.22 = (f16[52,32,128]{2,1,0:T(8,128)(2,1)}, f16[52,32,128]{2,1,0:T(8,128)(2,1)}, u32[]{:S(2)}, u32[]{:S(2)}) collective-permute-start(f16[52,32,128]{2,1,0:T(8,128)(2,1)} %get-tuple-element.104), channel_id=1, source_target_pairs={{0,2},{1,3},{2,0},{3,1},{4,6},{5,7},{6,4},{7,5},{8,10},{9,11},{10,... | collective-permute-start | bytes 1277960 | tf_op jit(solution)/shard_map/ppermute | solution.py:30
  83.9 21.0 %slice-start = ((s8[4718592]{0:T(1024)(128)(4,1)}), s8[4194304]{0:T(1024)(128)(4,1)S(1)}, s32[]{:S(2)}) async-start(s8[4718592]{0:T(1024)(128)(4,1)} %bitcast.70), calls=%async_computation.1 | async-start | bytes 8388608
  85.6 9.9 %collective-permute-start.26 = (bf16[52,32,128]{2,1,0:T(8,128)(2,1)S(1)}, bf16[52,32,128]{2,1,0:T(8,128)(2,1)S(1)}, u32[]{:S(2)}, u32[]{:S(2)}) collective-permute-start(bf16[52,32,128]{2,1,0:T(8,128)(2,1)S(1)} %fusion.40.refs_0_), channel_id=1, source_target_pairs={{0,1},{1,2},{2,3},{3,0},{4,5},{5,6},{6,7},{7,4},{8,9},{9,10},{10,1... | collective-permute-start | bytes 1277960 | tf_op jit(solution)/shard_map/ppermute | solution.py:30
  86.6 14.9 %collective-permute-start.25 = (bf16[52,32,128]{2,1,0:T(8,128)(2,1)S(1)}, bf16[52,32,128]{2,1,0:T(8,128)(2,1)S(1)}, u32[]{:S(2)}, u32[]{:S(2)}) collective-permute-start(bf16[52,32,128]{2,1,0:T(8,128)(2,1)S(1)} %fusion.40.refs_0_), channel_id=1, source_target_pairs={{0,2},{1,3},{2,0},{3,1},{4,6},{5,7},{6,4},{7,5},{8,10},{9,11},{10,... | collective-permute-start | bytes 1277960 | tf_op jit(solution)/shard_map/ppermute | solution.py:30
  90.8 10.7 %collective-permute-start.24 = (bf16[52,32,128]{2,1,0:T(8,128)(2,1)S(1)}, bf16[52,32,128]{2,1,0:T(8,128)(2,1)S(1)}, u32[]{:S(2)}, u32[]{:S(2)}) collective-permute-start(bf16[52,32,128]{2,1,0:T(8,128)(2,1)S(1)} %fusion.40.refs_0_), channel_id=1, source_target_pairs={{0,3},{1,0},{2,1},{3,2},{4,7},{5,4},{6,5},{7,6},{8,11},{9,8},{10,9... | collective-permute-start | bytes 1277960 | tf_op jit(solution)/shard_map/ppermute | solution.py:30
  106.5 6.5 %collective-permute-start.27 = (bf16[256,1152]{1,0:T(8,128)(2,1)S(1)}, bf16[256,1152]{1,0:T(8,128)(2,1)S(1)}, u32[]{:S(2)}, u32[]{:S(2)}) collective-permute-start(bf16[256,1152]{1,0:T(8,128)(2,1)S(1)} %fusion.25), channel_id=1, source_target_pairs={{0,64},{64,0},{1,65},{65,1},{2,66},{66,2},{3,67},{67,3},{4,68},{68... | collective-permute-start | bytes 1769480 | tf_op jit(solution)/shard_map/ppermute | solution.py:30
  112.3 7.3 %collective-permute-start.28 = (bf16[768,1152]{1,0:T(8,128)(2,1)S(1)}, bf16[768,1152]{1,0:T(8,128)(2,1)S(1)}, u32[]{:S(2)}, u32[]{:S(2)}) collective-permute-start(bf16[768,1152]{1,0:T(8,128)(2,1)S(1)} %fusion.20), channel_id=1, source_target_pairs={{0,64},{64,0},{1,65},{65,1},{2,66},{66,2},{3,67},{67,3},{4,68},{68... | collective-permute-start | bytes 5308424 | tf_op jit(solution)/shard_map/ppermute | solution.py:30
  113.0 17.8 %collective-permute-start.29 = (bf16[256,1152]{1,0:T(8,128)(2,1)S(1)}, bf16[256,1152]{1,0:T(8,128)(2,1)S(1)}, u32[]{:S(2)}, u32[]{:S(2)}) collective-permute-start(bf16[256,1152]{1,0:T(8,128)(2,1)S(1)} %add_convert_fusion), channel_id=1, source_target_pairs={{0,128},{4,132},{128,0},{132,4},{1,129},{5,133},{129,1},{133,5},{2... | collective-permute-start | bytes 1769480 | tf_op jit(solution)/shard_map/ppermute | solution.py:30
  120.1 22.9 %collective-permute-start.30 = (bf16[256,1152]{1,0:T(8,128)(2,1)S(1)}, bf16[256,1152]{1,0:T(8,128)(2,1)S(1)}, u32[]{:S(2)}, u32[]{:S(2)}) collective-permute-start(bf16[256,1152]{1,0:T(8,128)(2,1)S(1)} %get-tuple-element.105), channel_id=1, source_target_pairs={{0,4},{4,128},{128,132},{132,0},{1,5},{5,129},{129,133},{133,1},{2... | collective-permute-start | bytes 1769480 | tf_op jit(solution)/shard_map/ppermute | solution.py:30
  120.2 22.8 %collective-permute-start.31 = (bf16[256,1152]{1,0:T(8,128)(2,1)S(1)}, bf16[256,1152]{1,0:T(8,128)(2,1)S(1)}, u32[]{:S(2)}, u32[]{:S(2)}) collective-permute-start(bf16[256,1152]{1,0:T(8,128)(2,1)S(1)} %get-tuple-element.106), channel_id=1, source_target_pairs={{0,132},{4,0},{128,4},{132,128},{1,133},{5,1},{129,5},{133,129},{2... | collective-permute-start | bytes 1769480 | tf_op jit(solution)/shard_map/ppermute | solution.py:30
  (7 other events, 89.8 us)

commit v3 on v2

--- a/solution.py
+++ b/solution.py
@@ -18,6 +18,7 @@
 EARLY = 10
 GROUP = 8
 UNROLL = 4
+W_WIDE = 512
 SCALE = 16.0
 F32 = jnp.float32
 BF16 = jnp.bfloat16
@@ -88,24 +89,40 @@
 
 def encode_kernel(count, lead, bounds, low, high, table, facts, *refs):
     shards, w_ref, refs = refs[:count], refs[count], refs[count + 1 :]
-    earlier, (out_ref, rows, lhs, sem, back_sem) = refs[:-5], refs[-5:]
+    earlier, (out_ref, rows, w_buf, lhs, sem, w_sem, back_sem) = refs[:-7], refs[-7:]
+    loads = []
+    if not lead:
+        loads = [
+            pltpu.make_async_copy(w_ref.at[:, pl.ds(i * W_WIDE, W_WIDE)], w_buf.at[i], w_sem.at[i]) for i in range(4)
+        ]
     copies = [pltpu.make_async_copy(s, rows.at[pl.ds(4 * i, 4)], sem.at[i]) for i, s in enumerate(shards)]
     copies += [pltpu.make_async_copy(e, out_ref, back_sem) for e in earlier]
-    for c in copies:
+    for c in copies + loads:
         c.start()
     for c in copies:
         c.wait()
 
+    def weights(index):
+        if lead:
+            return w_ref[:, pl.ds(pl.multiple_of(index * BLOCK, BLOCK), BLOCK)]
+        return w_buf[index >> 2, :, pl.ds(pl.multiple_of((index & 3) * BLOCK, BLOCK), BLOCK)]
+
     def block(index, carry):
+        if not lead:
+
+            @pl.when(index & 3 == 0)
+            def _():
+                at = index >> 2
+                pltpu.make_async_copy(w_ref.at[:, pl.ds(0, W_WIDE)], w_buf.at[at], w_sem.at[at]).wait()
+
         first = jnp.maximum(facts[bounds[0] * BPO + index], low)
         last = jnp.minimum(facts[bounds[1] * BPO + index], high)
-        column = pl.ds(pl.multiple_of(index * BLOCK, BLOCK), BLOCK)
 
         def group(g, carry):
             codes = [table[jnp.minimum(first + g * GROUP + u, last - 1)] for u in range(GROUP)]
             for u in range(GROUP):
                 lhs[pl.ds(u * TILE, TILE), :] = rows[(codes[u] & 63) - 4 * lead]
-            part = jnp.dot(lhs[...], w_ref[:, column], preferred_element_type=F32)
+            part = jnp.dot(lhs[...], weights(index), preferred_element_type=F32)
             for u in range(GROUP):
                 out_ref[(codes[u] >> 16) - low] = part[u * TILE : (u + 1) * TILE]
             return carry
@@ -125,12 +142,14 @@
         grid_spec=pltpu.PrefetchScalarGridSpec(
             num_scalar_prefetch=2,
             grid=(),
-            in_specs=[any_space] * count + [vmem] + [any_space] * len(earlier),
+            in_specs=[any_space] * count + [vmem if lead else pl.BlockSpec(memory_space=pltpu.HBM)] + [any_space] * len(earlier),
             out_specs=vmem,
             scratch_shapes=[
                 pltpu.VMEM((4 * count, TILE, WIDTH), BF16),
+                pltpu.VMEM((8, 128) if lead else (4, WIDTH, W_WIDE), BF16),
                 pltpu.VMEM((GROUP * TILE, WIDTH), BF16),
                 pltpu.SemaphoreType.DMA((count,)),
+                pltpu.SemaphoreType.DMA((4,)),
                 pltpu.SemaphoreType.DMA,
             ],
         ),
@@ -226,14 +245,15 @@
 def shards(resid, block_lists, threshold_level, w_enc, w_dec):
     places = {name: lax.axis_index(name) for name in ("yh", "core", "z", "yl", "x")}
     w_enc, w_dec = w_enc[0], w_dec[0]
+    w_hbm = pltpu.with_memory_space_constraint(w_enc, pltpu.HBM)
     thresholds = threshold_level[0].reshape(BPO, BLOCK)
     table, facts = make_table(block_lists[0], places)
     gathered, early = gather_tokens(
-        resid[0], lambda arrived: encode(0, (0, 1), 0, FAST, table, facts, arrived, w_enc)
+        resid[0], lambda arrived: encode(0, (0, 1), 0, FAST, table, facts, arrived, w_hbm)
     )
     pre = encode(EARLY, (1, 2), 0, FAST, table, facts, gathered[EARLY:], w_enc, early)
     pieces = activate(0, FAST, pre, table, thresholds, places)
-    more = lax.cond(facts[3 * BPO] > FAST, some_more, no_more, table, facts, thresholds, w_enc, places, *gathered)
+    more = lax.cond(facts[3 * BPO] > FAST, some_more, no_more, table, facts, thresholds, w_hbm, places, *gathered)
     acts = place(table, facts, pieces + (more,))
     return reduce_tokens(acts, w_dec)
 

time: 169 us -> 167 us (0.988)
  blocking collectives: 24.2 us -> 21.7 us
    all_to_all x1, blocking collectives: 24.2 us -> 21.7 us  [reduce_tokens(): lax.all_to_all(column.astype(BF16).reshape(8, TILE, WIDTH), 'z', 0, 0, ti...]
  transfers between devices with their start and end apart: 26 -> 26, of which waited for: 12 -> 13; matrix products, arithmetic and copies ran while one was open for 9% -> 9% of each run, Pallas kernels for 6% -> 6%
where the time goes in v3:
time: 167 us; the launch traced here: 165 us
  waiting for transfers between devices  63.8 us (38%)
  starting transfers between devices  38.3 us (23%)
  blocking collectives  21.7 us (13%)
  Pallas kernels  19.9 us (12%)
  matrix products  11.9 us (7%)
  other arithmetic  6.02 us (4%)
  local copies, waits for them, and re-layouts  2.69 us (2%)
    ppermute x26, waiting for transfers between devices, shift(): return lambda value: lax.ppermute(value, axis, pairs)  63.8 us
    ppermute x26, starting transfers between devices, shift(): return lambda value: lax.ppermute(value, axis, pairs)  38.3 us
    all_to_all x1, blocking collectives, reduce_tokens(): lax.all_to_all(column.astype(BF16).reshape(8, TILE, WIDTH), 'z', 0, 0, ti...  21.7 us
    pallas_call x2, Pallas kernels, encode(): pl.pallas_call(functools.partial(encode_kernel, count, lead, bounds, low,...  16.3 us
    dot_general x2, matrix products, reduce_tokens(): jnp.dot(acts[start:stop], w_dec, preferred_element_type=F32).astype(BF16)  5.73 us
    dot_general x2, matrix products, reduce_tokens(): jnp.dot(acts[half + start:half + stop], w_dec, preferred_element_type=F32)  5.73 us
    pallas_call x1, Pallas kernels, place(): pl.pallas_call(place_kernel, out_shape=jax.ShapeDtypeStruct((TILES * TILE...  3.62 us
  transfers between devices with their start and end apart: 26, of which 13 were waited for; matrix products, arithmetic and copies ran while one was open for 9% of the time, Pallas kernels for 6%

profile of v3, /device:TPU:8, one launch (start us, length us, event | category | flops | bytes accessed | tf_op | source)
XLA Modules:
  0.0 165.3 jit_solution(1064488571232756125)
XLA Ops:
  0.0 2.2 %collective-permute-start.12 = (bf16[128,1152]{1,0:T(8,128)(2,1)}, bf16[128,1152]{1,0:T(8,128)(2,1)S(1)}, u32[]{:S(2)}, u32[]{:S(2)}) collective-permute-start(bf16[128,1152]{1,0:T(8,128)(2,1)} %bitcast.72), channel_id=1, source_target_pairs={{0,4},{4,0},{1,5},{5,1},{2,6},{6,2},{3,7},{7,3},{8,12},{12,8},{9,1... | collective-permute-start | bytes 884744 | tf_op jit(solution)/shard_map/ppermute | solution.py:31
  2.4 3.9 %collective-permute-start.6 = (bf16[128,1152]{1,0:T(8,128)(2,1)}, bf16[128,1152]{1,0:T(8,128)(2,1)S(1)}, u32[]{:S(2)}, u32[]{:S(2)}) collective-permute-start(bf16[128,1152]{1,0:T(8,128)(2,1)} %bitcast.74), channel_id=1, source_target_pairs={{0,56},{8,0},{16,8},{24,16},{32,24},{40,32},{48,40},{56,48},{1,57}... | collective-permute-start | bytes 884744 | tf_op jit(solution)/shard_map/ppermute | solution.py:31
  7.7 5.5 %collective-permute-done.7 = bf16[128,1152]{1,0:T(8,128)(2,1)S(1)} collective-permute-done((bf16[128,1152]{1,0:T(8,128)(2,1)}, bf16[128,1152]{1,0:T(8,128)(2,1)S(1)}, u32[]{:S(2)}, u32[]{:S(2)}) %collective-permute-start.7) | collective-permute-done | bytes 294944 | tf_op jit(solution)/shard_map/ppermute | solution.py:31
  13.3 3.2 %collective-permute-start.8 = (bf16[128,1152]{1,0:T(8,128)(2,1)S(1)}, bf16[128,1152]{1,0:T(8,128)(2,1)S(1)}, u32[]{:S(2)}, u32[]{:S(2)}) collective-permute-start(bf16[128,1152]{1,0:T(8,128)(2,1)S(1)} %collective-permute-done.6), channel_id=1, source_target_pairs={{0,56},{8,0},{16,8},{24,16},{32,24},{40,32},{48,40},{56,48},{1,57}... | collective-permute-start | bytes 884744 | tf_op jit(solution)/shard_map/ppermute | solution.py:31
  16.7 1.6 collective-permute-start.13
  18.7 3.7 %collective-permute-done.9 = bf16[128,1152]{1,0:T(8,128)(2,1)S(1)} collective-permute-done((bf16[128,1152]{1,0:T(8,128)(2,1)S(1)}, bf16[128,1152]{1,0:T(8,128)(2,1)S(1)}, u32[]{:S(2)}, u32[]{:S(2)}) %collective-permute-start.9) | collective-permute-done | bytes 294944 | tf_op jit(solution)/shard_map/ppermute | solution.py:31
  22.4 3.2 %collective-permute-start.10 = (bf16[128,1152]{1,0:T(8,128)(2,1)S(1)}, bf16[128,1152]{1,0:T(8,128)(2,1)S(1)}, u32[]{:S(2)}, u32[]{:S(2)}) collective-permute-start(bf16[128,1152]{1,0:T(8,128)(2,1)S(1)} %collective-permute-done.8), channel_id=1, source_target_pairs={{0,56},{8,0},{16,8},{24,16},{32,24},{40,32},{48,40},{56,48},{1,57}... | collective-permute-start | bytes 884744 | tf_op jit(solution)/shard_map/ppermute | solution.py:31
  27.2 1.7 %collective-permute-start.17 = (bf16[128,1152]{1,0:T(8,128)(2,1)S(1)}, bf16[128,1152]{1,0:T(8,128)(2,1)S(1)}, u32[]{:S(2)}, u32[]{:S(2)}) collective-permute-start(bf16[128,1152]{1,0:T(8,128)(2,1)S(1)} %collective-permute-done.9), channel_id=1, source_target_pairs={{0,4},{4,0},{1,5},{5,1},{2,6},{6,2},{3,7},{7,3},{8,12},{12,8},{9,1... | collective-permute-start | bytes 884744 | tf_op jit(solution)/shard_map/ppermute | solution.py:31
  28.9 4.1 %collective-permute-done.14 = bf16[128,1152]{1,0:T(8,128)(2,1)S(1)} collective-permute-done((bf16[128,1152]{1,0:T(8,128)(2,1)S(1)}, bf16[128,1152]{1,0:T(8,128)(2,1)S(1)}, u32[]{:S(2)}, u32[]{:S(2)}) %collective-permute-start.14) | collective-permute-done | bytes 294944 | tf_op jit(solution)/shard_map/ppermute | solution.py:31
  33.4 1.5 collective-permute-start.15
  35.0 9.6 %encode.4.refs_7_ = f32[208,32,128]{2,1,0:T(8,128)S(1)} custom-call(s32[320]{0:T(512)S(1)} %multiply_add_fusion.table, s32[50]{0:T(128)S(1)} %concatenate.6.facts, bf16[4,32,1152]{2,1,0:T(8,128)(2,1)} %bitcast.75, bf16[4,32,1152]{2,1,0:T(8,128)(2,1)S(1)} %bitcast.81, bf16[4,32,1152]{2,1,0:T(8,128)(2,1)S(1)} %bitcast.79, bf16[4,32,1152]{2,1,0:T(8,128)(2,1)S(1)} %bitcast.85, ...), custom_call_target="tpu_custom_call" | custom-call | flops 5000000000 | bytes 4000000 | tf_op jit(solution)/shard_map/encode/pallas_call | solution.py:139
  45.4 3.3 %collective-permute-start.18 = (bf16[128,1152]{1,0:T(8,128)(2,1)S(1)}, bf16[128,1152]{1,0:T(8,128)(2,1)S(1)}, u32[]{:S(2)}, u32[]{:S(2)}) collective-permute-start(bf16[128,1152]{1,0:T(8,128)(2,1)S(1)} %collective-permute-done.16), channel_id=1, source_target_pairs={{0,56},{8,0},{16,8},{24,16},{32,24},{40,32},{48,40},{56,48},{1,57}... | collective-permute-start | bytes 884744 | tf_op jit(solution)/shard_map/ppermute | solution.py:31
  49.4 2.1 %collective-permute-done.20 = bf16[128,1152]{1,0:T(8,128)(2,1)S(1)} collective-permute-done((bf16[128,1152]{1,0:T(8,128)(2,1)S(1)}, bf16[128,1152]{1,0:T(8,128)(2,1)S(1)}, u32[]{:S(2)}, u32[]{:S(2)}) %collective-permute-start.20) | collective-permute-done | bytes 294944 | tf_op jit(solution)/shard_map/ppermute | solution.py:31
  53.0 3.7 %collective-permute-done.19 = bf16[128,1152]{1,0:T(8,128)(2,1)S(1)} collective-permute-done((bf16[128,1152]{1,0:T(8,128)(2,1)S(1)}, bf16[128,1152]{1,0:T(8,128)(2,1)S(1)}, u32[]{:S(2)}, u32[]{:S(2)}) %collective-permute-start.19) | collective-permute-done | bytes 294944 | tf_op jit(solution)/shard_map/ppermute | solution.py:31
  56.7 6.7 %encode.5 = f32[208,32,128]{2,1,0:T(8,128)S(1)} custom-call(s32[320]{0:T(512)S(1)} %multiply_add_fusion.table, s32[50]{0:T(128)S(1)} %concatenate.6.facts, bf16[4,32,1152]{2,1,0:T(8,128)(2,1)S(1)} %bitcast.61, bf16[4,32,1152]{2,1,0:T(8,128)(2,1)S(1)} %bitcast.59, bf16[4,32,1152]{2,1,0:T(8,128)(2,1)S(1)} %bitcast.57, bf16[4,32,1152]{2,1,0:T(8,128)(2,1)S(1)} %bitcast.65, ...), custom_call_target="tpu_custom_call" | custom-call | flops 3000000000 | bytes 4000000 | tf_op jit(solution)/shard_map/encode/pallas_call | solution.py:139
  66.1 1.7 %collective-permute-start.23 = (f16[52,32,128]{2,1,0:T(8,128)(2,1)}, f16[52,32,128]{2,1,0:T(8,128)(2,1)}, u32[]{:S(2)}, u32[]{:S(2)}) collective-permute-start(f16[52,32,128]{2,1,0:T(8,128)(2,1)} %get-tuple-element.103), channel_id=1, source_target_pairs={{0,3},{1,0},{2,1},{3,2},{4,7},{5,4},{6,5},{7,6},{8,11},{9,8},{10,9... | collective-permute-start | bytes 1277960 | tf_op jit(solution)/shard_map/ppermute | solution.py:31
  68.9 1.8 %collective-permute-start.22 = (f16[52,32,128]{2,1,0:T(8,128)(2,1)}, f16[52,32,128]{2,1,0:T(8,128)(2,1)}, u32[]{:S(2)}, u32[]{:S(2)}) collective-permute-start(f16[52,32,128]{2,1,0:T(8,128)(2,1)} %get-tuple-element.104), channel_id=1, source_target_pairs={{0,2},{1,3},{2,0},{3,1},{4,6},{5,7},{6,4},{7,5},{8,10},{9,11},{10,... | collective-permute-start | bytes 1277960 | tf_op jit(solution)/shard_map/ppermute | solution.py:31
  71.0 5.2 %collective-permute-done.21 = f16[52,32,128]{2,1,0:T(8,128)(2,1)} collective-permute-done((f16[52,32,128]{2,1,0:T(8,128)(2,1)}, f16[52,32,128]{2,1,0:T(8,128)(2,1)}, u32[]{:S(2)}, u32[]{:S(2)}) %collective-permute-start.21) | collective-permute-done | bytes 426016 | tf_op jit(solution)/shard_map/ppermute | solution.py:31
  76.2 7.5 %collective-permute-done.22 = f16[52,32,128]{2,1,0:T(8,128)(2,1)} collective-permute-done((f16[52,32,128]{2,1,0:T(8,128)(2,1)}, f16[52,32,128]{2,1,0:T(8,128)(2,1)}, u32[]{:S(2)}, u32[]{:S(2)}) %collective-permute-start.22) | collective-permute-done | bytes 426016 | tf_op jit(solution)/shard_map/ppermute | solution.py:31
  83.7 1.7 %fusion.40.refs_0_ = bf16[52,32,128]{2,1,0:T(8,128)(2,1)S(1)} fusion(f32[208,32,128]{2,1,0:T(8,128)S(1)} %encode.5, f16[52,32,128]{2,1,0:T(8,128)(2,1)} %collective-permute-done.23, f16[52,32,128]{2,1,0:T(8,128)(2,1)} %collective-permute-done.22, f16[52,32,128]{2,1,0:T(8,128)(2,1)} %collective-permute-done.21, f32[52,128]{1,0:T(8,128)S(1)} %fusion.42), kind=kLoop, calls=%fused_computation.53 | loop fusion | flops 2129920 | bytes 2582528 | tf_op jit(solution)/shard_map/convert_element_type | solution.py:210
  86.4 4.3 %collective-permute-start.25 = (bf16[52,32,128]{2,1,0:T(8,128)(2,1)S(1)}, bf16[52,32,128]{2,1,0:T(8,128)(2,1)S(1)}, u32[]{:S(2)}, u32[]{:S(2)}) collective-permute-start(bf16[52,32,128]{2,1,0:T(8,128)(2,1)S(1)} %fusion.40.refs_0_), channel_id=1, source_target_pairs={{0,2},{1,3},{2,0},{3,1},{4,6},{5,7},{6,4},{7,5},{8,10},{9,11},{10,... | collective-permute-start | bytes 1277960 | tf_op jit(solution)/shard_map/ppermute | solution.py:31
  90.7 4.6 %collective-permute-done.26.refs_3_ = bf16[52,32,128]{2,1,0:T(8,128)(2,1)S(1)} collective-permute-done((bf16[52,32,128]{2,1,0:T(8,128)(2,1)S(1)}, bf16[52,32,128]{2,1,0:T(8,128)(2,1)S(1)}, u32[]{:S(2)}, u32[]{:S(2)}) %collective-permute-start.26) | collective-permute-done | bytes 426016 | tf_op jit(solution)/shard_map/ppermute | solution.py:31
  95.3 6.0 %collective-permute-done.25.refs_2_ = bf16[52,32,128]{2,1,0:T(8,128)(2,1)S(1)} collective-permute-done((bf16[52,32,128]{2,1,0:T(8,128)(2,1)S(1)}, bf16[52,32,128]{2,1,0:T(8,128)(2,1)S(1)}, u32[]{:S(2)}, u32[]{:S(2)}) %collective-permute-start.25) | collective-permute-done | bytes 426016 | tf_op jit(solution)/shard_map/ppermute | solution.py:31
  101.3 3.6 %place.1 = bf16[2048,2048]{1,0:T(8,128)(2,1)S(1)} custom-call(s32[320]{0:T(512)S(1)} %multiply_add_fusion.table, s32[50]{0:T(128)S(1)} %concatenate.6.facts, bf16[52,32,128]{2,1,0:T(8,128)(2,1)S(1)} %fusion.40.refs_0_, bf16[52,32,128]{2,1,0:T(8,128)(2,1)S(1)} %collective-permute-done.24.refs_1_, bf16[52,32,128]{2,1,0:T(8,128)(2,1)S(1)} %collective-permute-done.25.refs_2_, ...), custom_call_target="tpu_custom_call" | custom-call | flops 1000000 | bytes 8000000 | tf_op jit(solution)/shard_map/place/pallas_call | solution.py:188
  105.0 1.5 fusion.25
  108.1 4.2 %fusion.20 = bf16[768,1152]{1,0:T(8,128)(2,1)S(1)} fusion(bf16[1,2048,1152]{2,1,0:T(8,128)(2,1)S(1)} %bitcast.71, bf16[2048,2048]{1,0:T(8,128)(2,1)S(1)} %place.1), kind=kOutput, calls=%fused_computation.28 | convolution fusion | flops 3624763392 | bytes 9633792 | tf_op jit(solution)/shard_map/dot_general | solution.py:227
  113.1 2.8 %collective-permute-start.29 = (bf16[256,1152]{1,0:T(8,128)(2,1)S(1)}, bf16[256,1152]{1,0:T(8,128)(2,1)S(1)}, u32[]{:S(2)}, u32[]{:S(2)}) collective-permute-start(bf16[256,1152]{1,0:T(8,128)(2,1)S(1)} %add_convert_fusion), channel_id=1, source_target_pairs={{0,128},{4,132},{128,0},{132,4},{1,129},{5,133},{129,1},{133,5},{2... | collective-permute-start | bytes 1769480 | tf_op jit(solution)/shard_map/ppermute | solution.py:31
  115.8 4.2 %fusion.12 = f32[768,1152]{1,0:T(8,128)S(1)} fusion(bf16[1,2048,1152]{2,1,0:T(8,128)(2,1)S(1)} %bitcast.71, bf16[2048,2048]{1,0:T(8,128)(2,1)S(1)} %place.1), kind=kOutput, calls=%fused_computation.19 | convolution fusion | flops 3623878656 | bytes 11403264 | tf_op jit(solution)/shard_map/dot_general | solution.py:233
  120.6 2.0 %collective-permute-start.31 = (bf16[256,1152]{1,0:T(8,128)(2,1)S(1)}, bf16[256,1152]{1,0:T(8,128)(2,1)S(1)}, u32[]{:S(2)}, u32[]{:S(2)}) collective-permute-start(bf16[256,1152]{1,0:T(8,128)(2,1)S(1)} %get-tuple-element.106), channel_id=1, source_target_pairs={{0,132},{4,0},{128,4},{132,128},{1,133},{5,1},{129,5},{133,129},{2... | collective-permute-start | bytes 1769480 | tf_op jit(solution)/shard_map/ppermute | solution.py:31
  122.6 8.2 %collective-permute-done.29 = bf16[256,1152]{1,0:T(8,128)(2,1)S(1)} collective-permute-done((bf16[256,1152]{1,0:T(8,128)(2,1)S(1)}, bf16[256,1152]{1,0:T(8,128)(2,1)S(1)}, u32[]{:S(2)}, u32[]{:S(2)}) %collective-permute-start.29) | collective-permute-done | bytes 589856 | tf_op jit(solution)/shard_map/ppermute | solution.py:31
  130.9 11.1 %collective-permute-done.30 = bf16[256,1152]{1,0:T(8,128)(2,1)S(1)} collective-permute-done((bf16[256,1152]{1,0:T(8,128)(2,1)S(1)}, bf16[256,1152]{1,0:T(8,128)(2,1)S(1)}, u32[]{:S(2)}, u32[]{:S(2)}) %collective-permute-start.30) | collective-permute-done | bytes 589856 | tf_op jit(solution)/shard_map/ppermute | solution.py:31
  142.8 21.7 %all_to_all.5 = bf16[8,32,1152]{2,1,0:T(8,128)(2,1)S(1)} all-to-all(bf16[8,32,1152]{2,1,0:T(8,128)(2,1)S(1)} %bitcast.56), channel_id=1, replica_groups=mesh['yh'=2,'core'=2,'z'=8,'yl'=2,'x'=4] {'z'}, dimensions={0} | all-to-all | bytes 1179648 | tf_op jit(solution)/shard_map/all_to_all | solution.py:241
  (82 shorter events, 17.0 us)
Async XLA Ops:
  0.0 27.2 %collective-permute-start.12 = (bf16[128,1152]{1,0:T(8,128)(2,1)}, bf16[128,1152]{1,0:T(8,128)(2,1)S(1)}, u32[]{:S(2)}, u32[]{:S(2)}) collective-permute-start(bf16[128,1152]{1,0:T(8,128)(2,1)} %bitcast.72), channel_id=1, source_target_pairs={{0,4},{4,0},{1,5},{5,1},{2,6},{6,2},{3,7},{7,3},{8,12},{12,8},{9,1... | collective-permute-start | bytes 884744 | tf_op jit(solution)/shard_map/ppermute | solution.py:31
  2.2 11.1 %collective-permute-start.7 = (bf16[128,1152]{1,0:T(8,128)(2,1)}, bf16[128,1152]{1,0:T(8,128)(2,1)S(1)}, u32[]{:S(2)}, u32[]{:S(2)}) collective-permute-start(bf16[128,1152]{1,0:T(8,128)(2,1)} %bitcast.73), channel_id=1, source_target_pairs={{0,8},{8,16},{16,24},{24,32},{32,40},{40,48},{48,56},{56,0},{1,9},... | collective-permute-start | bytes 884744 | tf_op jit(solution)/shard_map/ppermute | solution.py:31
  2.4 10.9 %collective-permute-start.6 = (bf16[128,1152]{1,0:T(8,128)(2,1)}, bf16[128,1152]{1,0:T(8,128)(2,1)S(1)}, u32[]{:S(2)}, u32[]{:S(2)}) collective-permute-start(bf16[128,1152]{1,0:T(8,128)(2,1)} %bitcast.74), channel_id=1, source_target_pairs={{0,56},{8,0},{16,8},{24,16},{32,24},{40,32},{48,40},{56,48},{1,57}... | collective-permute-start | bytes 884744 | tf_op jit(solution)/shard_map/ppermute | solution.py:31
  13.3 31.3 %copy-start.4 = (bf16[128,1152]{1,0:T(8,128)(2,1)}, bf16[128,1152]{1,0:T(8,128)(2,1)S(1)}, u32[]{:S(2)}) copy-start(bf16[128,1152]{1,0:T(8,128)(2,1)S(1)} %collective-permute-done.7) | copy-start | bytes 884740
  13.3 9.1 %collective-permute-start.9 = (bf16[128,1152]{1,0:T(8,128)(2,1)S(1)}, bf16[128,1152]{1,0:T(8,128)(2,1)S(1)}, u32[]{:S(2)}, u32[]{:S(2)}) collective-permute-start(bf16[128,1152]{1,0:T(8,128)(2,1)S(1)} %collective-permute-done.7), channel_id=1, source_target_pairs={{0,8},{8,16},{16,24},{24,32},{32,40},{40,48},{48,56},{56,0},{1,9},... | collective-permute-start | bytes 884744 | tf_op jit(solution)/shard_map/ppermute | solution.py:31
  13.3 31.3 %copy-start.5 = (bf16[128,1152]{1,0:T(8,128)(2,1)}, bf16[128,1152]{1,0:T(8,128)(2,1)S(1)}, u32[]{:S(2)}) copy-start(bf16[128,1152]{1,0:T(8,128)(2,1)S(1)} %collective-permute-done.6) | copy-start | bytes 884740
  13.3 9.1 %collective-permute-start.8 = (bf16[128,1152]{1,0:T(8,128)(2,1)S(1)}, bf16[128,1152]{1,0:T(8,128)(2,1)S(1)}, u32[]{:S(2)}, u32[]{:S(2)}) collective-permute-start(bf16[128,1152]{1,0:T(8,128)(2,1)S(1)} %collective-permute-done.6), channel_id=1, source_target_pairs={{0,56},{8,0},{16,8},{24,16},{32,24},{40,32},{48,40},{56,48},{1,57}... | collective-permute-start | bytes 884744 | tf_op jit(solution)/shard_map/ppermute | solution.py:31
  16.7 18.3 %collective-permute-start.13 = (bf16[128,1152]{1,0:T(8,128)(2,1)S(1)}, bf16[128,1152]{1,0:T(8,128)(2,1)S(1)}, u32[]{:S(2)}, u32[]{:S(2)}) collective-permute-start(bf16[128,1152]{1,0:T(8,128)(2,1)S(1)} %collective-permute-done.7), channel_id=1, source_target_pairs={{0,4},{4,0},{1,5},{5,1},{2,6},{6,2},{3,7},{7,3},{8,12},{12,8},{9,1... | collective-permute-start | bytes 884744 | tf_op jit(solution)/shard_map/ppermute | solution.py:31
  18.2 14.7 %collective-permute-start.14 = (bf16[128,1152]{1,0:T(8,128)(2,1)S(1)}, bf16[128,1152]{1,0:T(8,128)(2,1)S(1)}, u32[]{:S(2)}, u32[]{:S(2)}) collective-permute-start(bf16[128,1152]{1,0:T(8,128)(2,1)S(1)} %collective-permute-done.6), channel_id=1, source_target_pairs={{0,4},{4,0},{1,5},{5,1},{2,6},{6,2},{3,7},{7,3},{8,12},{12,8},{9,1... | collective-permute-start | bytes 884744 | tf_op jit(solution)/shard_map/ppermute | solution.py:31
  22.4 22.3 %copy-start.6 = (bf16[128,1152]{1,0:T(8,128)(2,1)}, bf16[128,1152]{1,0:T(8,128)(2,1)S(1)}, u32[]{:S(2)}) copy-start(bf16[128,1152]{1,0:T(8,128)(2,1)S(1)} %collective-permute-done.9) | copy-start | bytes 884740
  22.4 11.1 %collective-permute-start.11 = (bf16[128,1152]{1,0:T(8,128)(2,1)S(1)}, bf16[128,1152]{1,0:T(8,128)(2,1)S(1)}, u32[]{:S(2)}, u32[]{:S(2)}) collective-permute-start(bf16[128,1152]{1,0:T(8,128)(2,1)S(1)} %collective-permute-done.9), channel_id=1, source_target_pairs={{0,8},{8,16},{16,24},{24,32},{32,40},{40,48},{48,56},{56,0},{1,9},... | collective-permute-start | bytes 884744 | tf_op jit(solution)/shard_map/ppermute | solution.py:31
  22.4 22.3 %copy-start.7 = (bf16[128,1152]{1,0:T(8,128)(2,1)}, bf16[128,1152]{1,0:T(8,128)(2,1)S(1)}, u32[]{:S(2)}) copy-start(bf16[128,1152]{1,0:T(8,128)(2,1)S(1)} %collective-permute-done.8) | copy-start | bytes 884740
  22.4 12.6 %collective-permute-start.10 = (bf16[128,1152]{1,0:T(8,128)(2,1)S(1)}, bf16[128,1152]{1,0:T(8,128)(2,1)S(1)}, u32[]{:S(2)}, u32[]{:S(2)}) collective-permute-start(bf16[128,1152]{1,0:T(8,128)(2,1)S(1)} %collective-permute-done.8), channel_id=1, source_target_pairs={{0,56},{8,0},{16,8},{24,16},{32,24},{40,32},{48,40},{56,48},{1,57}... | collective-permute-start | bytes 884744 | tf_op jit(solution)/shard_map/ppermute | solution.py:31
  27.2 17.5 %collective-permute-start.17 = (bf16[128,1152]{1,0:T(8,128)(2,1)S(1)}, bf16[128,1152]{1,0:T(8,128)(2,1)S(1)}, u32[]{:S(2)}, u32[]{:S(2)}) collective-permute-start(bf16[128,1152]{1,0:T(8,128)(2,1)S(1)} %collective-permute-done.9), channel_id=1, source_target_pairs={{0,4},{4,0},{1,5},{5,1},{2,6},{6,2},{3,7},{7,3},{8,12},{12,8},{9,1... | collective-permute-start | bytes 884744 | tf_op jit(solution)/shard_map/ppermute | solution.py:31
  32.9 11.8 %collective-permute-start.16 = (bf16[128,1152]{1,0:T(8,128)(2,1)S(1)}, bf16[128,1152]{1,0:T(8,128)(2,1)S(1)}, u32[]{:S(2)}, u32[]{:S(2)}) collective-permute-start(bf16[128,1152]{1,0:T(8,128)(2,1)S(1)} %collective-permute-done.14), channel_id=1, source_target_pairs={{0,56},{8,0},{16,8},{24,16},{32,24},{40,32},{48,40},{56,48},{1,57}... | collective-permute-start | bytes 884744 | tf_op jit(solution)/shard_map/ppermute | solution.py:31
  33.4 11.3 %collective-permute-start.15 = (bf16[128,1152]{1,0:T(8,128)(2,1)S(1)}, bf16[128,1152]{1,0:T(8,128)(2,1)S(1)}, u32[]{:S(2)}, u32[]{:S(2)}) collective-permute-start(bf16[128,1152]{1,0:T(8,128)(2,1)S(1)} %collective-permute-done.11), channel_id=1, source_target_pairs={{0,8},{8,16},{16,24},{24,32},{32,40},{40,48},{48,56},{56,0},{1,9},... | collective-permute-start | bytes 884744 | tf_op jit(solution)/shard_map/ppermute | solution.py:31
  35.0 21.7 %copy-start.1 = (bf16[1,1152,2048]{2,1,0:T(8,128)(2,1)S(1)}, bf16[1,1152,2048]{2,1,0:T(8,128)(2,1)}, u32[]{:S(2)}) copy-start(bf16[1,1152,2048]{2,1,0:T(8,128)(2,1)} %param.10) | copy-start | bytes 14155780
  44.7 6.8 %collective-permute-start.20 = (bf16[128,1152]{1,0:T(8,128)(2,1)S(1)}, bf16[128,1152]{1,0:T(8,128)(2,1)S(1)}, u32[]{:S(2)}, u32[]{:S(2)}) collective-permute-start(bf16[128,1152]{1,0:T(8,128)(2,1)S(1)} %collective-permute-done.15), channel_id=1, source_target_pairs={{0,4},{4,0},{1,5},{5,1},{2,6},{6,2},{3,7},{7,3},{8,12},{12,8},{9,1... | collective-permute-start | bytes 884744 | tf_op jit(solution)/shard_map/ppermute | solution.py:31
  45.4 7.6 %collective-permute-start.18 = (bf16[128,1152]{1,0:T(8,128)(2,1)S(1)}, bf16[128,1152]{1,0:T(8,128)(2,1)S(1)}, u32[]{:S(2)}, u32[]{:S(2)}) collective-permute-start(bf16[128,1152]{1,0:T(8,128)(2,1)S(1)} %collective-permute-done.16), channel_id=1, source_target_pairs={{0,56},{8,0},{16,8},{24,16},{32,24},{40,32},{48,40},{56,48},{1,57}... | collective-permute-start | bytes 884744 | tf_op jit(solution)/shard_map/ppermute | solution.py:31
  48.8 7.9 %collective-permute-start.19 = (bf16[128,1152]{1,0:T(8,128)(2,1)S(1)}, bf16[128,1152]{1,0:T(8,128)(2,1)S(1)}, u32[]{:S(2)}, u32[]{:S(2)}) collective-permute-start(bf16[128,1152]{1,0:T(8,128)(2,1)S(1)} %collective-permute-done.17), channel_id=1, source_target_pairs={{0,8},{8,16},{16,24},{24,32},{32,40},{40,48},{48,56},{56,0},{1,9},... | collective-permute-start | bytes 884744 | tf_op jit(solution)/shard_map/ppermute | solution.py:31
  64.6 11.6 %collective-permute-start.21 = (f16[52,32,128]{2,1,0:T(8,128)(2,1)}, f16[52,32,128]{2,1,0:T(8,128)(2,1)}, u32[]{:S(2)}, u32[]{:S(2)}) collective-permute-start(f16[52,32,128]{2,1,0:T(8,128)(2,1)} %get-tuple-element.102), channel_id=1, source_target_pairs={{0,1},{1,2},{2,3},{3,0},{4,5},{5,6},{6,7},{7,4},{8,9},{9,10},{10,1... | collective-permute-start | bytes 1277960 | tf_op jit(solution)/shard_map/ppermute | solution.py:31
  66.1 10.1 %collective-permute-start.23 = (f16[52,32,128]{2,1,0:T(8,128)(2,1)}, f16[52,32,128]{2,1,0:T(8,128)(2,1)}, u32[]{:S(2)}, u32[]{:S(2)}) collective-permute-start(f16[52,32,128]{2,1,0:T(8,128)(2,1)} %get-tuple-element.103), channel_id=1, source_target_pairs={{0,3},{1,0},{2,1},{3,2},{4,7},{5,4},{6,5},{7,6},{8,11},{9,8},{10,9... | collective-permute-start | bytes 1277960 | tf_op jit(solution)/shard_map/ppermute | solution.py:31
  68.9 14.7 %collective-permute-start.22 = (f16[52,32,128]{2,1,0:T(8,128)(2,1)}, f16[52,32,128]{2,1,0:T(8,128)(2,1)}, u32[]{:S(2)}, u32[]{:S(2)}) collective-permute-start(f16[52,32,128]{2,1,0:T(8,128)(2,1)} %get-tuple-element.104), channel_id=1, source_target_pairs={{0,2},{1,3},{2,0},{3,1},{4,6},{5,7},{6,4},{7,5},{8,10},{9,11},{10,... | collective-permute-start | bytes 1277960 | tf_op jit(solution)/shard_map/ppermute | solution.py:31
  83.7 21.3 %slice-start = ((s8[4718592]{0:T(1024)(128)(4,1)}), s8[4194304]{0:T(1024)(128)(4,1)S(1)}, s32[]{:S(2)}) async-start(s8[4718592]{0:T(1024)(128)(4,1)} %bitcast.70), calls=%async_computation.1 | async-start | bytes 8388608
  85.4 9.9 %collective-permute-start.26 = (bf16[52,32,128]{2,1,0:T(8,128)(2,1)S(1)}, bf16[52,32,128]{2,1,0:T(8,128)(2,1)S(1)}, u32[]{:S(2)}, u32[]{:S(2)}) collective-permute-start(bf16[52,32,128]{2,1,0:T(8,128)(2,1)S(1)} %fusion.40.refs_0_), channel_id=1, source_target_pairs={{0,1},{1,2},{2,3},{3,0},{4,5},{5,6},{6,7},{7,4},{8,9},{9,10},{10,1... | collective-permute-start | bytes 1277960 | tf_op jit(solution)/shard_map/ppermute | solution.py:31
  86.4 15.0 %collective-permute-start.25 = (bf16[52,32,128]{2,1,0:T(8,128)(2,1)S(1)}, bf16[52,32,128]{2,1,0:T(8,128)(2,1)S(1)}, u32[]{:S(2)}, u32[]{:S(2)}) collective-permute-start(bf16[52,32,128]{2,1,0:T(8,128)(2,1)S(1)} %fusion.40.refs_0_), channel_id=1, source_target_pairs={{0,2},{1,3},{2,0},{3,1},{4,6},{5,7},{6,4},{7,5},{8,10},{9,11},{10,... | collective-permute-start | bytes 1277960 | tf_op jit(solution)/shard_map/ppermute | solution.py:31
  90.7 10.7 %collective-permute-start.24 = (bf16[52,32,128]{2,1,0:T(8,128)(2,1)S(1)}, bf16[52,32,128]{2,1,0:T(8,128)(2,1)S(1)}, u32[]{:S(2)}, u32[]{:S(2)}) collective-permute-start(bf16[52,32,128]{2,1,0:T(8,128)(2,1)S(1)} %fusion.40.refs_0_), channel_id=1, source_target_pairs={{0,3},{1,0},{2,1},{3,2},{4,7},{5,4},{6,5},{7,6},{8,11},{9,8},{10,9... | collective-permute-start | bytes 1277960 | tf_op jit(solution)/shard_map/ppermute | solution.py:31
  106.5 6.4 %collective-permute-start.27 = (bf16[256,1152]{1,0:T(8,128)(2,1)S(1)}, bf16[256,1152]{1,0:T(8,128)(2,1)S(1)}, u32[]{:S(2)}, u32[]{:S(2)}) collective-permute-start(bf16[256,1152]{1,0:T(8,128)(2,1)S(1)} %fusion.25), channel_id=1, source_target_pairs={{0,64},{64,0},{1,65},{65,1},{2,66},{66,2},{3,67},{67,3},{4,68},{68... | collective-permute-start | bytes 1769480 | tf_op jit(solution)/shard_map/ppermute | solution.py:31
  112.4 7.7 %collective-permute-start.28 = (bf16[768,1152]{1,0:T(8,128)(2,1)S(1)}, bf16[768,1152]{1,0:T(8,128)(2,1)S(1)}, u32[]{:S(2)}, u32[]{:S(2)}) collective-permute-start(bf16[768,1152]{1,0:T(8,128)(2,1)S(1)} %fusion.20), channel_id=1, source_target_pairs={{0,64},{64,0},{1,65},{65,1},{2,66},{66,2},{3,67},{67,3},{4,68},{68... | collective-permute-start | bytes 5308424 | tf_op jit(solution)/shard_map/ppermute | solution.py:31
  113.1 17.8 %collective-permute-start.29 = (bf16[256,1152]{1,0:T(8,128)(2,1)S(1)}, bf16[256,1152]{1,0:T(8,128)(2,1)S(1)}, u32[]{:S(2)}, u32[]{:S(2)}) collective-permute-start(bf16[256,1152]{1,0:T(8,128)(2,1)S(1)} %add_convert_fusion), channel_id=1, source_target_pairs={{0,128},{4,132},{128,0},{132,4},{1,129},{5,133},{129,1},{133,5},{2... | collective-permute-start | bytes 1769480 | tf_op jit(solution)/shard_map/ppermute | solution.py:31
  120.5 21.5 %collective-permute-start.30 = (bf16[256,1152]{1,0:T(8,128)(2,1)S(1)}, bf16[256,1152]{1,0:T(8,128)(2,1)S(1)}, u32[]{:S(2)}, u32[]{:S(2)}) collective-permute-start(bf16[256,1152]{1,0:T(8,128)(2,1)S(1)} %get-tuple-element.105), channel_id=1, source_target_pairs={{0,4},{4,128},{128,132},{132,0},{1,5},{5,129},{129,133},{133,1},{2... | collective-permute-start | bytes 1769480 | tf_op jit(solution)/shard_map/ppermute | solution.py:31
  120.6 21.9 %collective-permute-start.31 = (bf16[256,1152]{1,0:T(8,128)(2,1)S(1)}, bf16[256,1152]{1,0:T(8,128)(2,1)S(1)}, u32[]{:S(2)}, u32[]{:S(2)}) collective-permute-start(bf16[256,1152]{1,0:T(8,128)(2,1)S(1)} %get-tuple-element.106), channel_id=1, source_target_pairs={{0,132},{4,0},{128,4},{132,128},{1,133},{5,1},{129,5},{133,129},{2... | collective-permute-start | bytes 1769480 | tf_op jit(solution)/shard_map/ppermute | solution.py:31
  (7 other events, 83.9 us)
